TPU v7x, 128 devices: a whole 4x4x4 slice. The times are simulated.
128 devices in a mesh: gz: 2 (over core), row: 4 (over x), col: 16 (over z, y).
Axes of the slice: x: 4, y: 4, z: 4, core: 2. Of those that a mesh axis runs over, the one named last changes fastest.
Arguments:
- right_side: float32 [4, 64, 16384], P(None, 'col', 'row'), may hold values from -6 to 6
- layer_sums: float32 [2, 4, 64, 16384], P('gz', None, 'col', 'row'), may hold values from -6 to 6
- lower_blocks: float32 [6, 64, 256, 256], P(None, 'col', 'row'), may hold values from -0.1875 to 0.1875
- upper_blocks: float32 [6, 64, 256, 256], P(None, 'col', 'row'), may hold values from -0.1875 to 0.1875
- lower_inverse: float32 [4, 64, 256, 256], P(None, 'col'), may hold values from -1 to 2, as said below
- upper_diagonal_inverses: float32 [4, 64, 256, 256], P(None, 'col'), may hold values from -1 to 2
- pattern: int32 [6, 64], P(None, 'col'), may hold values 0 or 1
- parents: int32 [3, 64], replicated, may hold values from 0 to 63
Outputs:
- forward_solution: float32 [4, 64, 16384], P(None, 'col')
- solution: float32 [4, 64, 16384], P(None, 'col')
Inputs may be any that keep to these rules, and one draw needn't show every extreme that they name: `lower_inverse`: inverses of the diagonal blocks of L.
All inputs are finite; a program needn't handle non-finite values. No bound on the sum of `pattern` on one device may be relied on, other than what follows from the above.
Results may differ from a plain program's by a relative error of at most 0.00013.
Values sent between devices are 32-bit elements; how exact they have to be, the bound alone decides.
A program may use at most 128 MiB of HBM per device.

v0:
```python
import jax
import jax.numpy as jnp
from jax import lax
from jax.sharding import PartitionSpec as P

WIDTH = 256
COLUMNS = 64


def place_of(height, distance):
    return height * (height - 1) // 2 + distance - 1


def solve_nodes(pieces, inverse):
    full_rows = lax.all_gather(pieces, "row", axis=1, tiled=True)
    return jnp.einsum("jvw,jwk->jvk", inverse, full_rows, precision=lax.Precision.HIGHEST)


def body(
    right_side,
    layer_sums,
    lower_blocks,
    upper_blocks,
    lower_inverse,
    upper_diagonal_inverses,
    pattern,
    parents,
):
    per_column = right_side.shape[1]
    part_rows = lower_blocks.shape[2]
    node_count = parents.shape[1]
    grid_column = lax.axis_index("col")
    present = pattern.astype(jnp.float32)
    node_range = jnp.arange(node_count, dtype=jnp.int32)
    picker_masks = {}
    for height in range(1, 4):
        current = lax.dynamic_slice_in_dim(
            parents[height - 1], grid_column * per_column, per_column, 0
        )
        for distance in range(1, height + 1):
            if distance > 1:
                lookup = parents[height - distance]
                current = jnp.sum(
                    jnp.where(current[:, None] == node_range[None, :], lookup[None, :], 0), axis=1
                )
            picker_masks[height, distance] = (current[:, None] == node_range[None, :]).astype(
                jnp.float32
            )
    shaped_right = right_side.reshape(4, per_column, part_rows, COLUMNS)
    own_columns = COLUMNS
    subtree_total = lax.psum(layer_sums[0], "gz").reshape(4, per_column, part_rows, COLUMNS)
    initial = shaped_right - subtree_total
    forward = [None] * 4
    received = [jnp.zeros((per_column, part_rows, own_columns), jnp.float32) for height in range(4)]
    for height in (3, 2, 1, 0):
        incoming = received[height]
        solved = solve_nodes(initial[height] - incoming, lower_inverse[height])
        forward[height] = solved
        summand_terms = []
        for distance in range(1, height + 1):
            block_place = place_of(height, distance)
            product = jnp.einsum(
                "jvw,jwk->jvk", lower_blocks[block_place], solved, precision=lax.Precision.HIGHEST
            )
            product = product * present[block_place][:, None, None]
            summand_terms.append(
                jnp.einsum(
                    "ja,jvk->avk",
                    picker_masks[height, distance],
                    product,
                    precision=lax.Precision.HIGHEST,
                )
            )
        if height > 0:
            gathered = lax.psum_scatter(
                jnp.stack(summand_terms, 1), "col", scatter_dimension=0, tiled=True
            )
            for distance in range(1, height + 1):
                received[height - distance] = (
                    received[height - distance] + gathered[:, distance - 1]
                )
    backward = [None] * 4
    whole_levels = [None] * 3
    row_start = lax.axis_index("row") * part_rows
    for height in range(4):
        remaining_right = lax.dynamic_slice_in_dim(forward[height], row_start, part_rows, 1)
        for distance in range(1, height + 1):
            block_place = place_of(height, distance)
            chosen = jnp.einsum(
                "ja,awk->jwk",
                picker_masks[height, distance],
                whole_levels[height - distance],
                precision=lax.Precision.HIGHEST,
            )
            update = jnp.einsum(
                "jvw,jwk->jvk", upper_blocks[block_place], chosen, precision=lax.Precision.HIGHEST
            )
            remaining_right = remaining_right - update * present[block_place][:, None, None]
        solved = solve_nodes(remaining_right, upper_diagonal_inverses[height])
        backward[height] = solved
        if height < 3:
            whole_levels[height] = lax.all_gather(solved, "col", axis=0, tiled=True)
    forward_all = jnp.stack(forward)
    backward_sweep_levels = jnp.stack(backward)
    return (
        forward_all.reshape(4, per_column, WIDTH * COLUMNS),
        backward_sweep_levels.reshape(4, per_column, WIDTH * COLUMNS),
    )


def solution(mesh):
    in_specs = (
        P(None, "col", "row"),
        P("gz", None, "col", "row"),
        P(None, "col", "row", None),
        P(None, "col", "row", None),
        P(None, "col", None, None),
        P(None, "col", None, None),
        P(None, "col"),
        P(),
    )
    out_specs = (P(None, "col", None), P(None, "col", None))
    return jax.shard_map(body, mesh=mesh, in_specs=in_specs, out_specs=out_specs, check_vma=False)
```

profile of v0, /device:TPU:1, one launch (start us, length us, event | category | flops | bytes accessed | tf_op | source)
XLA Modules:
  0.0 612.5 jit_solution(17601885622377758576)
XLA Ops:
  10.2 27.7 %all-reduce.2.cloned.1.call-done = f32[4,4,4096]{2,1,0:T(4,128)} async-done(((f32[4,4,4096]{2,1,0:T(4,128)}), f32[4,4,4096]{2,1,0:T(4,128)}) %all-reduce.2.cloned.1.call-update) | async-done | bytes 262160 | tf_op jit(solution)/shard_map/psum | solution.py:51
  39.2 11.1 %all_gather.33 = f32[4,256,64]{2,0,1:T(4,128)S(1)} all-gather(f32[4,64,64]{2,0,1:T(4,128)S(1)} %copy.40), channel_id=1, replica_groups=mesh['gz'=2,'row'=4,'col'=16] {'row'}, dimensions={1}, use_global_device_ids=true | all-gather | bytes 327680 | tf_op jit(solution)/shard_map/all_gather | solution.py:15
  50.3 2.4 fusion.37
  58.9 6.3 %copy.45 = f32[64,3,64,64]{3,2,1,0:T(8,128)} copy(f32[64,3,64,64]{3,0,2,1:T(8,128)S(1)} %pad_maximum_fusion) | data formatting | bytes 6291456 | tf_op jit(solution)/shard_map/stack | solution.py:76
  65.4 82.8 %reduce-scatter.4.cloned.1.call-done = f32[4,3,64,64]{3,2,1,0:T(8,128)} async-done(((f32[64,3,64,64]{3,2,1,0:T(8,128)}), f32[4,3,64,64]{3,2,1,0:T(8,128)}) %reduce-scatter.4.cloned.1.call-update) | async-done | bytes 196624 | tf_op jit(solution)/shard_map/reduce_scatter | solution.py:75
  149.2 10.6 %all_gather.34 = f32[4,256,64]{2,0,1:T(4,128)S(1)} all-gather(f32[4,64,64]{2,0,1:T(4,128)S(1)} %copy.48), channel_id=1, replica_groups=mesh['gz'=2,'row'=4,'col'=16] {'row'}, dimensions={1}, use_global_device_ids=true | all-gather | bytes 327680 | tf_op jit(solution)/shard_map/all_gather | solution.py:15
  159.8 2.4 fusion.35
  166.2 4.4 copy.52
  170.8 79.9 %reduce-scatter.6.cloned.1.call-done = f32[4,2,64,64]{3,2,1,0:T(8,128)} async-done(((f32[64,2,64,64]{3,2,1,0:T(8,128)}), f32[4,2,64,64]{3,2,1,0:T(8,128)}) %reduce-scatter.6.cloned.1.call-update) | async-done | bytes 131088 | tf_op jit(solution)/shard_map/reduce_scatter | solution.py:75
  251.8 10.3 %all_gather.35 = f32[4,256,64]{2,0,1:T(4,128)S(1)} all-gather(f32[4,64,64]{2,0,1:T(4,128)S(1)} %copy.56), channel_id=1, replica_groups=mesh['gz'=2,'row'=4,'col'=16] {'row'}, dimensions={1}, use_global_device_ids=true | all-gather | bytes 327680 | tf_op jit(solution)/shard_map/all_gather | solution.py:15
  262.1 2.4 fusion.33
  266.1 2.6 copy.59
  268.9 76.8 %reduce-scatter.8.cloned.1.call-done = f32[4,1,64,64]{3,2,1,0:T(8,128)} async-done(((f32[64,1,64,64]{3,2,1,0:T(8,128)}), f32[4,1,64,64]{3,2,1,0:T(8,128)}) %reduce-scatter.8.cloned.1.call-update) | async-done | bytes 65552 | tf_op jit(solution)/shard_map/reduce_scatter | solution.py:75
  346.8 10.8 %all_gather.36 = f32[4,256,64]{2,0,1:T(4,128)S(1)} all-gather(f32[4,64,64]{2,0,1:T(4,128)S(1)} %copy.61), channel_id=1, replica_groups=mesh['gz'=2,'row'=4,'col'=16] {'row'}, dimensions={1}, use_global_device_ids=true | all-gather | bytes 327680 | tf_op jit(solution)/shard_map/all_gather | solution.py:15
  357.6 2.4 fusion.31
  360.2 10.9 %all_gather.37 = f32[4,256,64]{2,0,1:T(4,128)S(1)} all-gather(f32[4,64,64]{2,0,1:T(4,128)S(1)} %copy.67), channel_id=1, replica_groups=mesh['gz'=2,'row'=4,'col'=16] {'row'}, dimensions={1}, use_global_device_ids=true | all-gather | bytes 327680 | tf_op jit(solution)/shard_map/all_gather | solution.py:15
  371.1 3.1 convolution_bitcast_fusion.9
  374.3 56.7 %all-gather.4.cloned.1.call-done = f32[64,256,64]{1,2,0:T(8,128)} async-done(((f32[4,256,64]{1,2,0:T(8,128)}), f32[64,256,64]{1,2,0:T(8,128)}) %all-gather.4.cloned.1.call-update) | async-done | bytes 4194320 | tf_op jit(solution)/shard_map/all_gather | solution.py:102
  430.9 5.8 fusion.10
  438.2 11.7 %all_gather.39 = f32[4,256,64]{2,0,1:T(4,128)S(1)} all-gather(f32[4,64,64]{2,0,1:T(4,128)S(1)} %copy.72), channel_id=1, replica_groups=mesh['gz'=2,'row'=4,'col'=16] {'row'}, dimensions={1}, use_global_device_ids=true | all-gather | bytes 327680 | tf_op jit(solution)/shard_map/all_gather | solution.py:15
  449.8 3.1 convolution_bitcast_fusion.8
  453.2 5.8 fusion.8
  458.9 46.8 %all-gather.6.cloned.1.call-done = f32[64,256,64]{1,2,0:T(8,128)} async-done(((f32[4,256,64]{1,2,0:T(8,128)}), f32[64,256,64]{1,2,0:T(8,128)}) %all-gather.6.cloned.1.call-update) | async-done | bytes 4194320 | tf_op jit(solution)/shard_map/all_gather | solution.py:102
  505.7 5.8 fusion.4
  514.4 11.9 %all_gather.41 = f32[4,256,64]{2,0,1:T(4,128)S(1)} all-gather(f32[4,64,64]{2,0,1:T(4,128)S(1)} %copy.79), channel_id=1, replica_groups=mesh['gz'=2,'row'=4,'col'=16] {'row'}, dimensions={1}, use_global_device_ids=true | all-gather | bytes 327680 | tf_op jit(solution)/shard_map/all_gather | solution.py:15
  526.2 3.1 convolution_bitcast_fusion.7
  533.2 5.8 fusion.6
  539.4 6.0 fusion.2
  545.5 36.7 %all-gather.8.cloned.1.call-done = f32[64,256,64]{1,2,0:T(8,128)} async-done(((f32[4,256,64]{1,2,0:T(8,128)}), f32[64,256,64]{1,2,0:T(8,128)}) %all-gather.8.cloned.1.call-update) | async-done | bytes 4194320 | tf_op jit(solution)/shard_map/all_gather | solution.py:102
  582.1 6.0 fusion
  589.5 11.7 %all_gather.43 = f32[4,256,64]{2,0,1:T(4,128)S(1)} all-gather(f32[4,64,64]{2,0,1:T(4,128)S(1)} %copy.88), channel_id=1, replica_groups=mesh['gz'=2,'row'=4,'col'=16] {'row'}, dimensions={1}, use_global_device_ids=true | all-gather | bytes 327680 | tf_op jit(solution)/shard_map/all_gather | solution.py:15
  601.1 2.4 convolution_bitcast_fusion.6
  (97 shorter events, 31.6 us)
Async XLA Ops:
  7.2 45.5 %copy-start.3 = (f32[6,4,64,256]{3,2,1,0:T(8,128)S(1)}, f32[6,4,64,256]{3,2,1,0:T(8,128)}, u32[]{:S(2)}) copy-start(f32[6,4,64,256]{3,2,1,0:T(8,128)} %param.10) | copy-start | bytes 4718596
  7.2 30.7 %all-reduce.2.cloned.1.call-start = ((), (), s32[]{:S(2)}) async-start(), calls=%async_computation.3 | async-start | bytes 524288 | tf_op jit(solution)/shard_map/psum | solution.py:51
  7.9 140.3 %reduce-scatter.4.cloned.1.call-start = ((), (), s32[]{:S(2)}) async-start(), calls=%async_computation.4 | async-start | bytes 6684672 | tf_op jit(solution)/shard_map/reduce_scatter | solution.py:75
  65.2 185.6 %reduce-scatter.6.cloned.1.call-start = ((), (), s32[]{:S(2)}) async-start(), calls=%async_computation.5 | async-start | bytes 4456448 | tf_op jit(solution)/shard_map/reduce_scatter | solution.py:75
  170.5 80.2 %copy-start.5 = (f32[4,3,64,64]{3,2,1,0:T(8,128)S(1)}, f32[4,3,64,64]{3,2,1,0:T(8,128)}, u32[]{:S(2)}) copy-start(f32[4,3,64,64]{3,2,1,0:T(8,128)} %reduce-scatter.4.cloned.1.call-done) | copy-start | bytes 589828
  170.6 175.2 %reduce-scatter.8.cloned.1.call-start = ((), (), s32[]{:S(2)}) async-start(), calls=%async_computation.6 | async-start | bytes 2228224 | tf_op jit(solution)/shard_map/reduce_scatter | solution.py:75
  265.0 80.8 %copy-start.6 = (f32[4,2,64,64]{3,2,1,0:T(8,128)S(1)}, f32[4,2,64,64]{3,2,1,0:T(8,128)}, u32[]{:S(2)}) copy-start(f32[4,2,64,64]{3,2,1,0:T(8,128)} %reduce-scatter.6.cloned.1.call-done) | copy-start | bytes 393220
  268.7 162.2 %all-gather.4.cloned.1.call-start = ((), (), s32[]{:S(2)}) async-start(), calls=%async_computation.7 | async-start | bytes 4456448 | tf_op jit(solution)/shard_map/all_gather | solution.py:102
  374.2 131.5 %all-gather.6.cloned.1.call-start = ((), (), s32[]{:S(2)}) async-start(), calls=%async_computation.8 | async-start | bytes 4456448 | tf_op jit(solution)/shard_map/all_gather | solution.py:102
  452.9 129.2 %all-gather.8.cloned.1.call-start = ((), (), s32[]{:S(2)}) async-start(), calls=%async_computation.9 | async-start | bytes 4456448 | tf_op jit(solution)/shard_map/all_gather | solution.py:102
  512.8 17.8 %copy-start = (f32[4,256,64]{1,2,0:T(8,128)S(1)}, f32[4,256,64]{1,2,0:T(8,128)}, u32[]{:S(2)}) copy-start(f32[4,256,64]{1,2,0:T(8,128)} %convolution_bitcast_fusion.9) | copy-start | bytes 786436
  529.8 3.0 copy-start.1
  531.5 7.4 %copy-start.2 = (f32[4,256,64]{1,2,0:T(8,128)S(1)}, f32[4,256,64]{1,2,0:T(8,128)}, u32[]{:S(2)}) copy-start(f32[4,256,64]{1,2,0:T(8,128)} %convolution_bitcast_fusion.7) | copy-start | bytes 786436
  539.4 48.7 %copy-start.4 = (f32[6,4,64,256]{3,2,1,0:T(8,128)S(1)}, f32[6,4,64,256]{3,2,1,0:T(8,128)}, u32[]{:S(2)}) copy-start(f32[6,4,64,256]{3,2,1,0:T(8,128)} %param.11) | copy-start | bytes 4718596
Sparse Core Ops, SparseCore 0:
  10.4 27.4 all-reduce.1
  65.3 82.8 reduce-scatter.3
  170.7 80.0 reduce-scatter.5
  268.9 76.8 reduce-scatter.7
  374.3 56.5 all-gather.3
  453.1 52.6 all-gather.5
  529.5 52.6 all-gather.7
where the time goes:
time: 622 us; the launch traced here: 612 us
  waiting for transfers between devices  408 us (66%)
  blocking collectives  88.9 us (14%)
  matrix products  70.5 us (11%)
  local copies, waits for them, and re-layouts  19.9 us (3%)
  between operations  15 us (2%)
  other arithmetic  9.55 us (2%)
    reduce_scatter x3, waiting for transfers between devices, body(): lax.psum_scatter(jnp.stack(summand_terms, 1), 'col', scatter_dimension=0,...  240 us
    all_gather x3, waiting for transfers between devices, body(): whole_levels[height] = lax.all_gather(solved, 'col', axis=0, tiled=True)  140 us
    all_gather x8, blocking collectives, solve_nodes(): full_rows = lax.all_gather(pieces, 'row', axis=1, tiled=True)  88.9 us
    dot_general x6, matrix products, body(): jnp.einsum('ja,awk->jwk', picker_masks[height, distance], whole_levels[he...  35.1 us
    psum x1, waiting for transfers between devices, body(): lax.psum(layer_sums[0], 'gz').reshape(4, per_column, part_rows, COLUMNS)  27.7 us
    dot_general x8, matrix products, solve_nodes(): jnp.einsum('jvw,jwk->jvk', inverse, full_rows, precision=lax.Precision.HI...  21.2 us
    another operation x3, local copies, waits for them, and re-layouts, body(): jnp.stack(summand_terms, 1)  13.2 us
  transfers between devices with their start and end apart: 7, of which 7 were waited for; matrix products, arithmetic and copies ran while one was open for 4% of the time, Pallas kernels for 0%

commit v1 on v0

v1 whole, which is shorter than its diff:
```python
import jax
import jax.numpy as jnp
from jax import lax
from jax.experimental import pallas as pl
from jax.experimental.pallas import tpu as pltpu
from jax.sharding import PartitionSpec as P

MESH = pl.DeviceIdType.MESH
F32 = jnp.float32
BF16 = jnp.bfloat16
LANES = 128
PART = 64
NODES_HERE = 4
OFFSETS = sorted(
    [(dz, dy) for dz in range(4) for dy in range(4) if dz or dy],
    key=lambda o: -(min(o[0], 4 - o[0]) + min(o[1], 4 - o[1])),
)
GZ_TOP, GZ_REST, ROW_IN, SCATTER, GATHER, ROW_OUT, FWD_OUT, BWD_OUT, U_SWAP, PHASES = (
    0, 1, 2, 6, 9, 12, 15, 19, 23, 24,
)
BLOCK = PART * LANES


def place_of(height, distance):
    return height * (height - 1) // 2 + distance - 1


def split(x):
    high = x.astype(BF16)
    return high, (x - high.astype(F32)).astype(BF16)


def dot(a, b):
    return jnp.dot(a, b, preferred_element_type=F32)


def pair_of(b):
    high, low = split(b)
    return high, jnp.concatenate([high, low], axis=1)


def product(a_high, a_low, b_pair):
    b_high, b_both = b_pair
    wide = dot(a_high, b_both)
    return wide[:, :LANES] + wide[:, LANES:] + dot(a_low, b_high)


def roll_groups(x, groups):
    groups = groups % 4
    return pltpu.roll(x, 32 * groups, 1) if groups else x


def kernel(
    right_hbm, sums_hbm, lower_hbm, upper_hbm, linv_hbm, uinv_hbm, pattern_ref, parents_ref,
    fwd_hbm, bwd_hbm,
    right, sums, lower, upper, linv, uinv,
    zsend, zrecv, init, rows_in, sbuf, qbuf, gbuf0, gbuf1, gbuf2, pbuf, prec,
    fbuf, ybuf, ustage, uswap, vhi, vlo, whi, wlo, ulhi, ullo, zpart, out_f, out_b,
    send_sem, recv_sem, load_sem, store_sem,
):
    g = lax.axis_index("gz")
    r = lax.axis_index("row")
    c = lax.axis_index("col")
    z, y = c // 4, c % 4
    gbuf = (gbuf0, gbuf1, gbuf2)

    def column(offset):
        return ((z + offset[0]) % 4) * 4 + (y + offset[1]) % 4

    loads = {}

    def load(name, source, target):
        loads[name] = pltpu.make_async_copy(source, target, load_sem.at[len(loads)])
        loads[name].start()

    load("right", right_hbm, right)
    load("sums", sums_hbm, sums)
    load("lower", lower_hbm, lower)
    load("linv3", linv_hbm.at[3], linv.at[3])
    load("linv2", linv_hbm.at[2], linv.at[2])
    load("upper", upper_hbm, upper)
    load("linv1", linv_hbm.at[1], linv.at[1])
    load("linv0", linv_hbm.at[0], linv.at[0])
    for height in (3, 0, 1, 2):
        load("uinv%d" % height, uinv_hbm.at[height], uinv.at[height])

    barrier = pltpu.get_barrier_semaphore()
    for offset in OFFSETS:
        pl.semaphore_signal(
            barrier, inc=1, device_id={"col": column(offset)}, device_id_type=MESH
        )
    others = []
    for step in range(4):
        others.append({"gz": 1 - g, "row": (r + step) % 4})
    for step in range(1, 4):
        others.append({"gz": g, "row": (r + step) % 4})
    for place in others:
        pl.semaphore_signal(barrier, inc=1, device_id=place, device_id_type=MESH)

    def send(source, target, phase, place):
        pltpu.make_async_remote_copy(
            src_ref=source, dst_ref=target, send_sem=send_sem.at[phase],
            recv_sem=recv_sem.at[phase], device_id=place, device_id_type=MESH,
        ).start()

    def wait_blocks(sem, blocks):
        whole = qbuf.at[0, pl.ds(0, blocks)] if blocks <= 16 else uswap.at[pl.ds(0, blocks // 12)]
        pltpu.make_async_copy(whole, whole, sem).wait()

    my_rows = pl.ds(pl.multiple_of(r * PART, PART), PART)
    row_steps = (2, 1, 3)

    ancestor, stored = {}, {}
    for height in (1, 2, 3):
        for m in range(NODES_HERE):
            current = parents_ref[height - 1, c * NODES_HERE + m]
            for distance in range(1, height + 1):
                if distance > 1:
                    current = parents_ref[height - distance, current]
                ancestor[height, distance, m] = current
                stored[height, distance, m] = pattern_ref[place_of(height, distance), m] != 0

    group = lax.broadcasted_iota(jnp.int32, (PART, LANES), 1) // 32

    def regroup(x, shift_of, rows):
        lanes = lax.broadcasted_iota(jnp.int32, (rows, LANES), 1) // 32
        total = None
        for m in range(4):
            block, source = shift_of(m)
            moved = roll_groups(x[block], m - source)
            total = moved if total is None else jnp.where(lanes == m, moved, total)
        return total

    def take_input(height):
        for parity in range(2):
            blocks_r = [right[pl.ds(height * 128 + m, 32, stride=4), :] for m in range(4)]
            blocks_s = [sums[pl.ds(height * 128 + m, 32, stride=4), :] for m in range(4)]
            diff = [a - b for a, b in zip(blocks_r, blocks_s)]
            halves_d = [regroup(diff, lambda m: (m, 2 * parity + half), 32) for half in range(2)]
            halves_s = [regroup(blocks_s, lambda m: (m, 2 * parity + half), 32) for half in range(2)]
            mine = pl.ds(parity, 32, stride=2)
            init[height, mine, :] = jnp.where(g == 0, halves_d[0], halves_d[1])
            zsend[height, mine, :] = jnp.where(g == 0, halves_s[1], halves_s[0])

    loads["right"].wait()
    loads["sums"].wait()
    take_input(3)
    pl.semaphore_wait(barrier, len(OFFSETS) + len(others))
    send(zsend.at[3], zrecv.at[3], GZ_TOP, {"gz": 1 - g})
    for height in (2, 1, 0):
        take_input(height)
    send(zsend.at[pl.ds(0, 3)], zrecv.at[pl.ds(0, 3)], GZ_REST, {"gz": 1 - g})

    def make_v(height):
        def one(m, carry):
            b_high, b_low = split(linv[height, m])
            for distance in range(1, height + 1):
                q = place_of(height, distance)
                a_high, a_low = split(lower[q, m])
                v_high, v_low = split(dot(a_high, b_high) + dot(a_high, b_low) + dot(a_low, b_high))
                vhi[q, m] = v_high
                vlo[q, m] = v_low
            return carry
        lax.fori_loop(0, NODES_HERE, one, 0)

    def share_rows(height, value):
        rows_in[height, my_rows, :] = value
        for step in row_steps:
            send(
                rows_in.at[height, my_rows, :], rows_in.at[height, my_rows, :],
                ROW_IN + height, {"row": (r + step) % 4},
            )

    def scatter_terms(height, distance, b_pair, first, out):
        q = place_of(height, distance)
        target = height - distance
        terms = []
        for m in range(NODES_HERE):
            own = product(vhi[q, m], vlo[q, m], b_pair)
            spread = own
            for t in range(4):
                if t != m:
                    spread = jnp.where(group == t, roll_groups(own, t - m), spread)
            terms.append(spread)
        wanted = [
            jnp.where(stored[height, distance, m], ancestor[height, distance, m], -1)
            for m in range(NODES_HERE)
        ]
        for offset in OFFSETS + [(0, 0)]:
            slot = offset[0] * 4 + offset[1]
            base = column(offset) * NODES_HERE
            total = jnp.zeros((PART, LANES), F32) if first else sbuf[target, slot]
            for m in range(NODES_HERE):
                total = total + jnp.where(group == wanted[m] - base, terms[m], 0.0)
            sbuf[target, slot] = total
            if out and slot:
                send(
                    sbuf.at[target, slot], qbuf.at[target, slot], SCATTER + target,
                    {"col": column(offset)},
                )

    def solve_into(inverse, height, b_pair, target):
        lanes = lax.broadcasted_iota(jnp.int32, (256, LANES), 1) // 32

        def one(m, carry):
            a_high, a_low = split(inverse[height, m])
            whole = product(a_high, a_low, b_pair)
            target[...] = jnp.where(lanes == m, whole, target[...])
            return carry

        target[...] = jnp.zeros((256, LANES), F32)
        lax.fori_loop(0, NODES_HERE, one, 0)

    def write_out(source, out, hbm, height, slot):
        lanes = lax.broadcasted_iota(jnp.int32, (128, LANES), 1) // 32
        pieces = [
            source[height, half, pl.ds(parity, 128, stride=2), :]
            for parity in range(2) for half in range(2)
        ]
        for m in range(NODES_HERE):
            total = None
            for place in range(4):
                moved = roll_groups(pieces[place], place - m)
                total = moved if total is None else jnp.where(lanes == place, moved, total)
            out[pl.ds(height * 512 + m, 128, stride=4), :] = total
        pltpu.make_async_copy(
            out.at[pl.ds(height * 512, 512)], hbm.at[pl.ds(height * 512, 512)], store_sem.at[slot]
        ).start()

    def sum_received(target):
        total = init[target] - sbuf[target, 0]
        for slot in range(1, 16):
            total = total - qbuf[target, slot]
        return total

    def stage_upper():
        lanes = lax.broadcasted_iota(jnp.int32, (PART, LANES), 1)

        def one(m, carry):
            for index, (first, second) in enumerate(((1, 2), (3, 4), (5, 0))):
                for part in range(4):
                    tile = slice(LANES * (part // 2), LANES * (part // 2) + LANES)
                    a, b = upper[first, m, :, tile], upper[second, m, :, tile]
                    if part % 2 == 0:
                        b = pltpu.roll(b, 64, 1)
                    else:
                        a = pltpu.roll(a, 64, 1)
                    ustage[part, index, m] = jnp.where(lanes < 64, a, b)
            return carry

        lax.fori_loop(0, NODES_HERE, one, 0)

    def make_w(height):
        pairs = {1: (2,), 2: (0,), 3: (1, 2)}[height]

        def one(m, carry):
            a_high, a_low = split(uinv[height, m])
            for place, index in enumerate(pairs):
                b = jnp.concatenate([uswap[part, index, m] for part in range(4)], axis=0)
                w_high, w_low = split(product(a_high, a_low, pair_of(b)))
                whi[height + place - 1, m] = w_high
                wlo[height + place - 1, m] = w_low
            return carry

        lax.fori_loop(0, NODES_HERE, one, 0)

    def make_z(height):
        b_pair = pair_of(fbuf[height, g])
        total = None
        for m in range(NODES_HERE):
            a_high, a_low = split(uinv[height, m, my_rows, :])
            own = product(a_high, a_low, b_pair)
            total = own if total is None else jnp.where(group == m, own, total)
        zpart[height - 1] = total

    def finish_forward(height, b_pair):
        solve_into(linv, height, b_pair, fbuf.at[height, g])
        send(fbuf.at[height, g], fbuf.at[height, g], FWD_OUT + height, {"gz": 1 - g})

    loads["lower"].wait()
    loads["linv3"].wait()
    make_v(3)
    wait_blocks(recv_sem.at[GZ_TOP], 1)
    share_rows(3, init[3] - zrecv[3])
    loads["upper"].wait()
    stage_upper()
    wait_blocks(recv_sem.at[ROW_IN + 3], 3)
    b_pair = pair_of(rows_in[3])
    scatter_terms(3, 1, b_pair, True, True)
    for step in row_steps:
        send(ustage.at[(r + step) % 4], uswap.at[r], U_SWAP, {"row": (r + step) % 4})
    own_upper = pltpu.make_async_copy(ustage.at[r], uswap.at[r], load_sem.at[len(loads)])
    own_upper.start()
    scatter_terms(3, 2, b_pair, True, False)
    scatter_terms(3, 3, b_pair, True, False)
    finish_forward(3, b_pair)
    loads["linv2"].wait()
    make_v(2)
    wait_blocks(recv_sem.at[GZ_REST], 3)
    for height in range(3):
        init[height] = init[height] - zrecv[height]

    wait_blocks(recv_sem.at[SCATTER + 2], 15)
    share_rows(2, sum_received(2))
    loads["linv1"].wait()
    make_v(1)
    wait_blocks(recv_sem.at[ROW_IN + 2], 3)
    b_pair = pair_of(rows_in[2])
    scatter_terms(2, 1, b_pair, False, True)
    scatter_terms(2, 2, b_pair, False, False)
    finish_forward(2, b_pair)
    loads["uinv3"].wait()
    make_z(3)
    wait_blocks(recv_sem.at[FWD_OUT + 3], 4)
    write_out(fbuf, out_f, fwd_hbm, 3, 0)

    wait_blocks(recv_sem.at[SCATTER + 1], 15)
    share_rows(1, sum_received(1))
    wait_blocks(recv_sem.at[ROW_IN + 1], 3)
    b_pair = pair_of(rows_in[1])
    scatter_terms(1, 1, b_pair, False, True)
    finish_forward(1, b_pair)
    loads["linv0"].wait()
    loads["uinv0"].wait()

    def make_ul(m, carry):
        b_high, b_low = split(linv[0, m])
        a_high, a_low = split(uinv[0, m, my_rows, :])
        ul_high, ul_low = split(dot(a_high, b_high) + dot(a_high, b_low) + dot(a_low, b_high))
        ulhi[m] = ul_high
        ullo[m] = ul_low
        return carry

    lax.fori_loop(0, NODES_HERE, make_ul, 0)
    loads["uinv1"].wait()
    loads["uinv2"].wait()
    wait_blocks(recv_sem.at[U_SWAP], 36)
    own_upper.wait()
    make_w(1)

    wait_blocks(recv_sem.at[SCATTER + 0], 15)
    share_rows(0, sum_received(0))
    make_z(2)
    wait_blocks(recv_sem.at[ROW_IN + 0], 3)
    b_pair = pair_of(rows_in[0])

    def share_solution(height, value):
        gbuf[height][0] = value
        for offset in OFFSETS:
            slot = offset[0] * 4 + offset[1]
            send(
                gbuf[height].at[0], gbuf[height].at[slot], GATHER + height,
                {"col": column(offset)},
            )

    top = None
    for m in range(NODES_HERE):
        own = product(ulhi[m], ullo[m], b_pair)
        top = own if top is None else jnp.where(group == m, own, top)
    share_solution(0, top)
    finish_forward(0, b_pair)
    make_z(1)
    solve_into(uinv, 0, pair_of(fbuf[0, g]), ybuf.at[0, g])
    send(ybuf.at[0, g], ybuf.at[0, g], BWD_OUT, {"gz": 1 - g})
    make_w(2)

    def chosen(height, distance):
        total = jnp.zeros((PART, LANES), F32)
        for m in range(NODES_HERE):
            a = ancestor[height, distance, m]
            chip = a // NODES_HERE
            slot = ((z + 4 - chip // 4) % 4) * 4 + (y + 4 - chip % 4) % 4
            block = gbuf[height - distance][slot]
            present = stored[height, distance, m]
            for source in range(4):
                here = jnp.where(jnp.logical_and(present, a % NODES_HERE == source), m, -1)
                total = jnp.where(group == here, roll_groups(block, m - source), total)
        return total

    row_lanes = lax.broadcasted_iota(jnp.int32, (256, LANES), 1) // 32

    def row_terms(height, pieces):
        zero = jnp.zeros((PART, LANES), F32)
        pieces = {1: [zero] + pieces, 2: pieces, 3: pieces + [zero]}[height]
        pairs = [pair_of(jnp.concatenate(pieces[i:i + 2], axis=0)) for i in range(0, len(pieces), 2)]

        def one(m, carry):
            whole = product(whi[height - 1, m], wlo[height - 1, m], pairs[0])
            if height == 3:
                whole = whole + product(whi[3, m], wlo[3, m], pairs[1])
            pbuf[height - 1] = jnp.where(row_lanes == m, whole, pbuf[height - 1])
            return carry

        pbuf[height - 1] = jnp.zeros((256, LANES), F32)
        for m in range(NODES_HERE):
            one(m, 0)
        for step in row_steps:
            to = (r + step) % 4
            send(
                pbuf.at[height - 1, pl.ds(pl.multiple_of(to * PART, PART), PART), :],
                prec.at[height - 1, step - 1], ROW_OUT + height - 1, {"row": to},
            )

    def take_rows(height):
        wait_blocks(recv_sem.at[ROW_OUT + height - 1], 3)
        total = zpart[height - 1] - pbuf[height - 1, my_rows, :]
        for step in range(3):
            total = total - prec[height - 1, step]
        return total

    def spread_out(height, value):
        ybuf[height, g, my_rows, :] = value
        for place in others:
            send(
                ybuf.at[height, g, my_rows, :], ybuf.at[height, g, my_rows, :],
                BWD_OUT + height, place,
            )

    wait_blocks(recv_sem.at[GATHER + 0], 15)
    row_terms(1, [chosen(1, 1)])
    wait_blocks(recv_sem.at[FWD_OUT + 2], 4)
    write_out(fbuf, out_f, fwd_hbm, 2, 1)
    value = take_rows(1)
    share_solution(1, value)
    spread_out(1, value)
    make_w(3)
    early2 = chosen(2, 2)
    early3 = chosen(3, 3)
    wait_blocks(recv_sem.at[FWD_OUT + 1], 4)
    write_out(fbuf, out_f, fwd_hbm, 1, 2)

    wait_blocks(recv_sem.at[GATHER + 1], 15)
    row_terms(2, [chosen(2, 1), early2])
    wait_blocks(recv_sem.at[FWD_OUT + 0], 4)
    write_out(fbuf, out_f, fwd_hbm, 0, 3)
    value = take_rows(2)
    share_solution(2, value)
    spread_out(2, value)
    early32 = chosen(3, 2)
    wait_blocks(recv_sem.at[BWD_OUT + 0], 4)
    write_out(ybuf, out_b, bwd_hbm, 0, 4)
    wait_blocks(recv_sem.at[BWD_OUT + 1], 7)
    write_out(ybuf, out_b, bwd_hbm, 1, 5)

    wait_blocks(recv_sem.at[GATHER + 2], 15)
    row_terms(3, [chosen(3, 1), early32, early3])
    wait_blocks(recv_sem.at[BWD_OUT + 2], 7)
    write_out(ybuf, out_b, bwd_hbm, 2, 6)
    spread_out(3, take_rows(3))
    wait_blocks(recv_sem.at[BWD_OUT + 3], 7)
    write_out(ybuf, out_b, bwd_hbm, 3, 7)

    for phase, blocks in (
        [(GZ_TOP, 1), (GZ_REST, 3), (U_SWAP, 36)]
        + [(ROW_IN + h, 3) for h in range(4)]
        + [(SCATTER + t, 15) for t in range(3)]
        + [(GATHER + t, 15) for t in range(3)]
        + [(ROW_OUT + h, 3) for h in range(3)]
        + [(FWD_OUT + h, 4) for h in range(4)]
        + [(BWD_OUT + h, 4 if h == 0 else 7) for h in range(4)]
    ):
        wait_blocks(send_sem.at[phase], blocks)
    for slot, (height, out, hbm) in enumerate(
        [(h, out_f, fwd_hbm) for h in (3, 2, 1, 0)] + [(h, out_b, bwd_hbm) for h in (0, 1, 2, 3)]
    ):
        rows = pl.ds(height * 512, 512)
        pltpu.make_async_copy(out.at[rows], hbm.at[rows], store_sem.at[slot]).wait()


def body(
    right_side, layer_sums, lower_blocks, upper_blocks, lower_inverse, upper_diagonal_inverses,
    pattern, parents,
):
    def tiled(x):
        return x.reshape(4, 4, 32, 128).transpose(0, 2, 1, 3).reshape(512, 128)

    anywhere = pl.BlockSpec(memory_space=pl.ANY)
    scalar = pl.BlockSpec(memory_space=pltpu.SMEM)
    forward, backward = pl.pallas_call(
        kernel,
        out_shape=[jax.ShapeDtypeStruct((2048, 128), F32)] * 2,
        in_specs=[anywhere] * 6 + [scalar] * 2,
        out_specs=[anywhere] * 2,
        scratch_shapes=[
            pltpu.VMEM((512, 128), F32),
            pltpu.VMEM((512, 128), F32),
            pltpu.VMEM((6, 4, 64, 256), F32),
            pltpu.VMEM((6, 4, 64, 256), F32),
            pltpu.VMEM((4, 4, 256, 256), F32),
            pltpu.VMEM((4, 4, 256, 256), F32),
            pltpu.VMEM((4, 64, 128), F32),
            pltpu.VMEM((4, 64, 128), F32),
            pltpu.VMEM((4, 64, 128), F32),
            pltpu.VMEM((4, 256, 128), F32),
            pltpu.VMEM((3, 16, 64, 128), F32),
            pltpu.VMEM((3, 16, 64, 128), F32),
            pltpu.VMEM((16, 64, 128), F32),
            pltpu.VMEM((16, 64, 128), F32),
            pltpu.VMEM((16, 64, 128), F32),
            pltpu.VMEM((3, 256, 128), F32),
            pltpu.VMEM((3, 3, 64, 128), F32),
            pltpu.VMEM((4, 2, 256, 128), F32),
            pltpu.VMEM((4, 2, 256, 128), F32),
            pltpu.VMEM((4, 3, 4, 64, 128), F32),
            pltpu.VMEM((4, 3, 4, 64, 128), F32),
            pltpu.VMEM((6, 4, 64, 256), BF16),
            pltpu.VMEM((6, 4, 64, 256), BF16),
            pltpu.VMEM((4, 4, 256, 128), BF16),
            pltpu.VMEM((4, 4, 256, 128), BF16),
            pltpu.VMEM((4, 64, 256), BF16),
            pltpu.VMEM((4, 64, 256), BF16),
            pltpu.VMEM((3, 64, 128), F32),
            pltpu.VMEM((2048, 128), F32),
            pltpu.VMEM((2048, 128), F32),
            pltpu.SemaphoreType.DMA((PHASES,)),
            pltpu.SemaphoreType.DMA((PHASES,)),
            pltpu.SemaphoreType.DMA((16,)),
            pltpu.SemaphoreType.DMA((8,)),
        ],
        compiler_params=pltpu.CompilerParams(
            collective_id=0, has_side_effects=True, vmem_limit_bytes=56 * 1024 * 1024
        ),
    )(
        tiled(right_side), tiled(layer_sums[0]), lower_blocks, upper_blocks, lower_inverse,
        upper_diagonal_inverses, pattern, parents,
    )

    def untiled(x):
        return x.reshape(4, 128, 4, 128).transpose(0, 2, 1, 3).reshape(4, 4, 16384)

    return untiled(forward), untiled(backward)


def solution(mesh):
    in_specs = (
        P(None, "col", "row"),
        P("gz", None, "col", "row"),
        P(None, "col", "row", None),
        P(None, "col", "row", None),
        P(None, "col", None, None),
        P(None, "col", None, None),
        P(None, "col"),
        P(),
    )
    out_specs = (P(None, "col", None), P(None, "col", None))
    return jax.shard_map(body, mesh=mesh, in_specs=in_specs, out_specs=out_specs, check_vma=False)
```

time: 622 us -> 105 us (0.17); the launches traced: 612 us -> 105 us
  waiting for transfers between devices: 408 us -> 0 us
  Pallas kernels: 0 us -> 98.1 us
  blocking collectives: 88.9 us -> 0 us
  matrix products: 70.5 us -> 0 us
  between operations: 15 us -> 0.64 us
  local copies, waits for them, and re-layouts: 19.9 us -> 5.88 us
  other arithmetic: 9.55 us -> 0 us
    reduce_scatter x3 -> x0, waiting for transfers between devices: 240 us -> none  [body(): lax.psum_scatter(jnp.stack(summand_terms, 1), 'col', scatter_dimension=0,...]
    all_gather x3 -> x0, waiting for transfers between devices: 140 us -> none  [body(): whole_levels[height] = lax.all_gather(solved, 'col', axis=0, tiled=True)]
    pallas_call x0 -> x1, Pallas kernels: none -> 98.1 us  [body(): pl.pallas_call(kernel, out_shape=[jax.ShapeDtypeStruct((2048, 128), F32)]...]
    all_gather x8 -> x0, blocking collectives: 88.9 us -> none  [solve_nodes(): full_rows = lax.all_gather(pieces, 'row', axis=1, tiled=True)]
    dot_general x32 -> x0, matrix products: 70.5 us -> none  [the longest x6 35.1 us: body(): jnp.einsum('ja,awk->jwk', picker_masks[height, distance], whole_levels[he...]
    psum x1 -> x0, waiting for transfers between devices: 27.7 us -> none  [body(): lax.psum(layer_sums[0], 'gz').reshape(4, per_column, part_rows, COLUMNS)]
    another operation x11 -> x0, local copies, waits for them, and re-layouts: 15.1 us -> none  [the longest x3 13.2 us: body(): jnp.stack(summand_terms, 1)]
  transfers between devices with their start and end apart: 7 -> 0, of which waited for: 7 -> 0; matrix products, arithmetic and copies ran while one was open for 4% -> 0% of each run, Pallas kernels for 0% -> 0%
where the time goes in v1:
time: 105 us
  Pallas kernels  98.1 us (93%)
  local copies, waits for them, and re-layouts  5.88 us (6%)
    pallas_call x1, Pallas kernels, body(): pl.pallas_call(kernel, out_shape=[jax.ShapeDtypeStruct((2048, 128), F32)]...  98.1 us
    unnamed x3, local copies, waits for them, and re-layouts  5.88 us

profile of v1, /device:TPU:1, one launch (start us, length us, event | category | flops | bytes accessed | tf_op | source)
XLA Modules:
  0.0 104.6 jit_solution(18022883300818054899)
XLA Ops:
  0.6 1.4 %copy.12.pattern_ref = s32[6,4]{1,0:T(8,128)} copy(s32[6,4]{0,1:T(4,128)} %param.14) | data formatting | bytes 192 | tf_op args[6]
  2.0 98.1 %shard_map.95 = (f32[2048,128]{1,0:T(8,128)}, f32[2048,128]{1,0:T(8,128)}) custom-call(f32[512,128]{1,0:T(8,128)} %bitcast.22, f32[512,128]{1,0:T(8,128)} %bitcast.23, f32[6,4,64,256]{3,2,1,0:T(8,128)} %lower_hbm.1, f32[6,4,64,256]{3,2,1,0:T(8,128)} %upper_hbm.1, f32[4,4,256,256]{3,2,1,0:T(8,128)} %linv_hbm.1, f32[4,4,256,256]{3,2,1,0:T(8,128)} %uinv_hbm.1, ...), custom_call_target="tpu_custom_call" | custom-call | tf_op jit(solution)/shard_map/pallas_call | solution.py:479
  100.1 2.3 %copy.17 = f32[4,4,16384]{2,1,0:T(4,128)} copy(f32[4,4,16384]{2,1,0:T(4,128)} %bitcast.21) | data formatting | bytes 2097152
  102.3 2.3 %copy.18 = f32[4,4,16384]{2,1,0:T(4,128)} copy(f32[4,4,16384]{2,1,0:T(4,128)} %bitcast.20) | data formatting | bytes 2097152

commit v2 on v0

v2 whole, which is shorter than its diff:
```python
import jax
import jax.numpy as jnp
from jax import lax
from jax.experimental import pallas as pl
from jax.experimental.pallas import tpu as pltpu
from jax.sharding import PartitionSpec as P

MESH = pl.DeviceIdType.MESH
F32 = jnp.float32
BF16 = jnp.bfloat16
LANES = 128
PART = 64
NODES_HERE = 4
OFFSETS = sorted(
    [(dz, dy) for dz in range(4) for dy in range(4) if dz or dy],
    key=lambda o: -(min(o[0], 4 - o[0]) + min(o[1], 4 - o[1])),
)
INPUT, SCATTER, GATHER, FWD_OUT, BWD_OUT, L_ROW, L_GZ, U_ROW, U_GZ, PHASES = (
    0, 1, 4, 7, 11, 15, 21, 27, 33, 39,
)


def place_of(height, distance):
    return height * (height - 1) // 2 + distance - 1


def lane_ids(rows):
    return lax.broadcasted_iota(jnp.int32, (rows, LANES), 1)


def split(x):
    high = x.astype(BF16)
    return high, (x - high.astype(F32)).astype(BF16)


def dot(a, b):
    return jnp.dot(a, b, preferred_element_type=F32)


def wide_of(a):
    return jnp.concatenate(split(a), axis=1)


def rolled(x, lanes):
    lanes = lanes % LANES
    return pltpu.roll(x, lanes, 1) if lanes else x


def operand_of(x):
    full = jnp.concatenate([rolled(x, -32 * part) for part in range(4)], axis=0)
    high = full.astype(BF16).astype(F32)
    low = full - high
    lanes = lane_ids(256)
    both = jnp.where(lanes < 32, high, rolled(low.astype(BF16).astype(F32), 32))
    alone = jnp.where(lanes < 32, high, 0.0)
    return jnp.concatenate([both.astype(BF16), alone.astype(BF16)], axis=0)


def apply(matrix_of, operand):
    node = (lane_ids(256) // 8) % 4
    total = None
    for m in range(NODES_HERE):
        out = dot(matrix_of(m), operand)
        total = out if total is None else jnp.where(node == m, out, total)
    total = total + rolled(total, -32)
    quarter = lane_ids(PART) // 32
    packed = None
    for part in range(4):
        moved = rolled(total[part * PART:(part + 1) * PART], 32 * part)
        packed = moved if packed is None else jnp.where(quarter == part, moved, packed)
    return packed


def exchange(arrays):
    octet = lane_ids(arrays[0].shape[0]) // 8
    arrays = list(arrays)
    for bit in (1, 2, 4, 8):
        low = (octet // bit) % 2 == 0
        for i in range(16):
            if i & bit:
                continue
            a, b = arrays[i], arrays[i | bit]
            arrays[i] = jnp.where(low, a, rolled(b, 8 * bit))
            arrays[i | bit] = jnp.where(low, rolled(a, -8 * bit), b)
    return arrays


def kernel(
    right_hbm, sums_hbm, lower_hbm, upper_hbm, linv_hbm, uinv_hbm, pattern_ref, parents_ref,
    fwd_hbm, bwd_hbm,
    right, sums, lower, upper, linv, uinv,
    xsend, xrecv, init, sbuf, qbuf, gbuf0, gbuf1, gbuf2,
    fbuf, ybuf, top_inv, v21, v11, ul, w11, w21, w31, out_f, out_b,
    send_sem, recv_sem, load_sem, store_sem,
):
    g = lax.axis_index("gz")
    r = lax.axis_index("row")
    c = lax.axis_index("col")
    z, y = c // 4, c % 4
    me = g * 4 + r
    gbuf = (gbuf0, gbuf1, gbuf2)

    def column(offset):
        return ((z + offset[0]) % 4) * 4 + (y + offset[1]) % 4

    loads = {}

    def load(name, source, target):
        loads[name] = pltpu.make_async_copy(source, target, load_sem.at[len(loads)])
        loads[name].start()

    my_rows = pl.ds(pl.multiple_of(r * PART, PART), PART)
    my_nodes = pl.ds(g * 2, 2)
    load("right", right_hbm, right)
    load("sums", sums_hbm, sums)
    load("linv3", linv_hbm.at[3], linv.at[3])
    load("lower", lower_hbm.at[:, my_nodes], lower.at[:, my_nodes, my_rows, :])
    load("linv2", linv_hbm.at[2], linv.at[2])
    load("linv1", linv_hbm.at[1], linv.at[1])
    load("upper", upper_hbm.at[:, my_nodes], upper.at[:, my_nodes, my_rows, :])
    load("linv0", linv_hbm.at[0], linv.at[0])
    for height in (0, 1, 2, 3):
        load("uinv%d" % height, uinv_hbm.at[height], uinv.at[height])

    barrier = pltpu.get_barrier_semaphore()
    for offset in OFFSETS:
        pl.semaphore_signal(
            barrier, inc=1, device_id={"col": column(offset)}, device_id_type=MESH
        )
    row_steps = (2, 1, 3)
    others = []
    for step in (2, 1, 3):
        others.append((g, (r + step) % 4))
        others.append((1 - g, (r + step) % 4))
    others.append((1 - g, r))
    for place in others:
        pl.semaphore_signal(
            barrier, inc=1, device_id={"gz": place[0], "row": place[1]}, device_id_type=MESH
        )

    def send(source, target, phase, place):
        pltpu.make_async_remote_copy(
            src_ref=source, dst_ref=target, send_sem=send_sem.at[phase],
            recv_sem=recv_sem.at[phase], device_id=place, device_id_type=MESH,
        ).start()

    def wait_bytes(whole, sem):
        pltpu.make_async_copy(whole, whole, sem).wait()

    def wait_blocks(sem, blocks):
        wait_bytes(qbuf.at[0, pl.ds(0, blocks)], sem)

    ancestor, stored = {}, {}
    for height in (1, 2, 3):
        for m in range(NODES_HERE):
            current = parents_ref[height - 1, c * NODES_HERE + m]
            for distance in range(1, height + 1):
                if distance > 1:
                    current = parents_ref[height - distance, current]
                ancestor[height, distance, m] = current
                stored[height, distance, m] = pattern_ref[m, place_of(height, distance)] != 0

    node_of = (lane_ids(PART) // 8) % 4

    def gather_matrix(source, target, phase, q):
        for step in row_steps:
            send(
                source.at[q, my_nodes], target.at[q, my_nodes, my_rows, :], phase + q,
                {"row": (r + step) % 4},
            )

    def hand_over(target, phase_row, phase_gz, q):
        wait_bytes(target.at[q, pl.ds(0, 2), pl.ds(0, 192), :], recv_sem.at[phase_row + q])
        send(target.at[q, my_nodes], target.at[q, my_nodes], phase_gz + q, {"gz": 1 - g})

    def wait_matrix(target, phase_gz, q):
        wait_bytes(target.at[q, pl.ds(0, 2)], recv_sem.at[phase_gz + q])

    def lower_send(q):
        gather_matrix(lower_hbm, lower, L_ROW, q)

    def upper_send(q):
        gather_matrix(upper_hbm, upper, U_ROW, q)

    def lower_hand(q):
        hand_over(lower, L_ROW, L_GZ, q)

    def upper_hand(q):
        hand_over(upper, U_ROW, U_GZ, q)

    def multiply(target, a_of, b_of):
        def one(m, carry):
            a_high, a_low = split(a_of(m))
            b_high, b_low = split(b_of(m))
            target[m] = wide_of(dot(a_high, b_high) + dot(a_high, b_low) + dot(a_low, b_high))
            return carry
        lax.fori_loop(0, NODES_HERE, one, 0)

    def scatter_terms(height, distance, product, first, out):
        target = height - distance
        moved = {shift: rolled(product, 8 * shift) for shift in range(-3, 4)}
        terms = []
        for m in range(NODES_HERE):
            spread = moved[-m]
            for t in range(1, 4):
                spread = jnp.where(node_of == t, moved[t - m], spread)
            terms.append(spread)
        wanted = [
            jnp.where(stored[height, distance, m], ancestor[height, distance, m], -1)
            for m in range(NODES_HERE)
        ]
        for offset in OFFSETS + [(0, 0)]:
            slot = offset[0] * 4 + offset[1]
            base = column(offset) * NODES_HERE
            total = jnp.zeros((PART, LANES), F32) if first else sbuf[target, slot]
            for m in range(NODES_HERE):
                total = total + jnp.where(node_of == wanted[m] - base, terms[m], 0.0)
            sbuf[target, slot] = total
            if out and slot:
                send(
                    sbuf.at[target, slot], qbuf.at[target, slot], SCATTER + target,
                    {"col": column(offset)},
                )

    def sum_received(target):
        wait_blocks(recv_sem.at[SCATTER + target], 15)
        total = init[target] - sbuf[target, 0]
        for slot in range(1, 16):
            total = total - qbuf[target, slot]
        return total

    def spread_out(buffer, phase, height, value):
        buffer[height, me] = value
        for place in others:
            send(
                buffer.at[height, me], buffer.at[height, me], phase + height,
                {"gz": place[0], "row": place[1]},
            )

    def write_out(buffer, phase, out, hbm, height, slot):
        wait_blocks(recv_sem.at[phase + height], 7)
        pieces = exchange([
            buffer[height, octet, pl.ds(parity, 32, stride=2), :]
            for parity in range(2) for octet in range(8)
        ])
        for index in range(16):
            part, m = index // 4, index % 4
            out[pl.ds(height * 512 + part * 128 + m, 32, stride=4), :] = pieces[index]
        rows = pl.ds(height * 512, 512)
        pltpu.make_async_copy(out.at[rows], hbm.at[rows], store_sem.at[slot]).start()

    def chosen(height, distance):
        total = jnp.zeros((PART, LANES), F32)
        for m in range(NODES_HERE):
            a = ancestor[height, distance, m]
            chip = a // NODES_HERE
            slot = ((z + 4 - chip // 4) % 4) * 4 + (y + 4 - chip % 4) % 4
            block = gbuf[height - distance][slot]
            present = stored[height, distance, m]
            for source in range(4):
                here = jnp.where(jnp.logical_and(present, a % NODES_HERE == source), m, -1)
                total = jnp.where(node_of == here, rolled(block, 8 * (m - source)), total)
        return total

    def share_solution(height, value):
        gbuf[height][0] = value
        for offset in OFFSETS:
            slot = offset[0] * 4 + offset[1]
            send(
                gbuf[height].at[0], gbuf[height].at[slot], GATHER + height,
                {"col": column(offset)},
            )

    loads["right"].wait()
    loads["sums"].wait()
    sources = []
    for height in range(4):
        for m in range(NODES_HERE):
            rows = pl.ds(height * 128 + m, 32, stride=4)
            sources.append(jnp.where(g == 0, right[rows, :], 0.0) - sums[rows, :])
    pieces = exchange(sources)
    for parity in range(2):
        for octet in range(8):
            xsend[octet, pl.ds(parity, 32, stride=2), :] = pieces[parity * 8 + octet]
    pl.semaphore_wait(barrier, len(OFFSETS) + len(others))
    for place in others:
        send(
            xsend.at[place[0] * 4 + place[1]], xrecv.at[me], INPUT,
            {"gz": place[0], "row": place[1]},
        )
    lower_send(3)
    xrecv[me] = xsend[me]
    loads["linv3"].wait()

    def widen_top(m, carry):
        top_inv[m] = wide_of(linv[3, m])
        return carry

    lax.fori_loop(0, NODES_HERE, widen_top, 0)
    lower_send(1)
    lower_send(4)
    wait_blocks(recv_sem.at[INPUT], 7)
    sums_of_part = [xrecv[part] + xrecv[4 + part] for part in range(4)]
    quarter = lane_ids(PART) // 32
    for height in (3, 2, 1, 0):
        total = None
        for part in range(4):
            moved = rolled(sums_of_part[part], 32 * (part - height))
            total = moved if total is None else jnp.where(quarter == part, moved, total)
        init[height] = total

    solved = apply(lambda m: top_inv[m], operand_of(init[3]))
    operand3 = operand_of(solved)
    loads["lower"].wait()
    lower_hand(3)
    wait_matrix(lower, L_GZ, 3)
    scatter_terms(3, 1, apply(lambda m: wide_of(lower[3, m]), operand3), True, True)
    spread_out(fbuf, FWD_OUT, 3, solved)
    for q in (0, 2, 5):
        lower_send(q)
    lower_hand(1)
    lower_hand(4)
    loads["linv2"].wait()
    wait_matrix(lower, L_GZ, 1)
    multiply(v21, lambda m: lower[1, m], lambda m: linv[2, m])
    wait_matrix(lower, L_GZ, 4)
    scatter_terms(3, 2, apply(lambda m: wide_of(lower[4, m]), operand3), True, False)

    operand = operand_of(sum_received(2))
    scatter_terms(2, 1, apply(lambda m: v21[m], operand), False, True)
    for q in (0, 2, 1):
        upper_send(q)
    lower_hand(0)
    lower_hand(2)
    lower_hand(5)
    loads["linv1"].wait()
    wait_matrix(lower, L_GZ, 0)
    multiply(v11, lambda m: lower[0, m], lambda m: linv[1, m])
    solved = apply(lambda m: wide_of(linv[2, m]), operand)
    spread_out(fbuf, FWD_OUT, 2, solved)
    wait_matrix(lower, L_GZ, 5)
    scatter_terms(3, 3, apply(lambda m: wide_of(lower[5, m]), operand3), True, False)
    wait_matrix(lower, L_GZ, 2)
    scatter_terms(2, 2, apply(lambda m: wide_of(lower[2, m]), operand_of(solved)), False, False)

    operand = operand_of(sum_received(1))
    scatter_terms(1, 1, apply(lambda m: v11[m], operand), False, True)
    for q in (5, 4, 3):
        upper_send(q)
    solved = apply(lambda m: wide_of(linv[1, m]), operand)
    spread_out(fbuf, FWD_OUT, 1, solved)
    loads["linv0"].wait()
    loads["uinv0"].wait()
    multiply(ul, lambda m: uinv[0, m], lambda m: linv[0, m])
    loads["uinv1"].wait()
    rest1 = apply(lambda m: wide_of(uinv[1, m]), operand_of(solved))
    loads["upper"].wait()
    upper_hand(0)

    operand = operand_of(sum_received(0))
    value = apply(lambda m: ul[m], operand)
    share_solution(0, value)
    spread_out(fbuf, FWD_OUT, 0, apply(lambda m: wide_of(linv[0, m]), operand))
    spread_out(ybuf, BWD_OUT, 0, value)
    wait_matrix(upper, U_GZ, 0)
    multiply(w11, lambda m: uinv[1, m], lambda m: upper[0, m])
    upper_hand(2)
    upper_hand(1)
    write_out(fbuf, FWD_OUT, out_f, fwd_hbm, 3, 0)
    write_out(fbuf, FWD_OUT, out_f, fwd_hbm, 2, 1)

    wait_blocks(recv_sem.at[GATHER + 0], 15)
    value = rest1 - apply(lambda m: w11[m], operand_of(chosen(1, 1)))
    share_solution(1, value)
    spread_out(ybuf, BWD_OUT, 1, value)
    wait_matrix(upper, U_GZ, 1)
    loads["uinv2"].wait()
    multiply(w21, lambda m: uinv[2, m], lambda m: upper[1, m])
    wait_matrix(upper, U_GZ, 2)
    rest = fbuf[2, me] - apply(lambda m: wide_of(upper[2, m]), operand_of(chosen(2, 2)))
    rest2 = apply(lambda m: wide_of(uinv[2, m]), operand_of(rest))
    upper_hand(5)
    write_out(fbuf, FWD_OUT, out_f, fwd_hbm, 1, 2)
    write_out(fbuf, FWD_OUT, out_f, fwd_hbm, 0, 3)

    wait_blocks(recv_sem.at[GATHER + 1], 15)
    value = rest2 - apply(lambda m: w21[m], operand_of(chosen(2, 1)))
    share_solution(2, value)
    spread_out(ybuf, BWD_OUT, 2, value)
    upper_hand(4)
    upper_hand(3)
    wait_matrix(upper, U_GZ, 5)
    rest = fbuf[3, me] - apply(lambda m: wide_of(upper[5, m]), operand_of(chosen(3, 3)))
    wait_matrix(upper, U_GZ, 4)
    rest = rest - apply(lambda m: wide_of(upper[4, m]), operand_of(chosen(3, 2)))
    loads["uinv3"].wait()
    rest3 = apply(lambda m: wide_of(uinv[3, m]), operand_of(rest))
    wait_matrix(upper, U_GZ, 3)
    multiply(w31, lambda m: uinv[3, m], lambda m: upper[3, m])
    write_out(ybuf, BWD_OUT, out_b, bwd_hbm, 0, 4)
    write_out(ybuf, BWD_OUT, out_b, bwd_hbm, 1, 5)

    wait_blocks(recv_sem.at[GATHER + 2], 15)
    value = rest3 - apply(lambda m: w31[m], operand_of(chosen(3, 1)))
    spread_out(ybuf, BWD_OUT, 3, value)
    write_out(ybuf, BWD_OUT, out_b, bwd_hbm, 2, 6)
    write_out(ybuf, BWD_OUT, out_b, bwd_hbm, 3, 7)

    for phase, blocks in (
        [(INPUT, 7)]
        + [(SCATTER + t, 15) for t in range(3)]
        + [(GATHER + t, 15) for t in range(3)]
        + [(FWD_OUT + h, 7) for h in range(4)]
        + [(BWD_OUT + h, 7) for h in range(4)]
    ):
        wait_blocks(send_sem.at[phase], blocks)
    for q in range(6):
        for phase_row, phase_gz in ((L_ROW, L_GZ), (U_ROW, U_GZ)):
            wait_bytes(lower.at[q, pl.ds(0, 2), pl.ds(0, 192), :], send_sem.at[phase_row + q])
            wait_bytes(lower.at[q, pl.ds(0, 2)], send_sem.at[phase_gz + q])
    for slot, (height, out, hbm) in enumerate(
        [(h, out_f, fwd_hbm) for h in (3, 2, 1, 0)] + [(h, out_b, bwd_hbm) for h in (0, 1, 2, 3)]
    ):
        rows = pl.ds(height * 512, 512)
        pltpu.make_async_copy(out.at[rows], hbm.at[rows], store_sem.at[slot]).wait()


def body(
    right_side, layer_sums, lower_blocks, upper_blocks, lower_inverse, upper_diagonal_inverses,
    pattern, parents,
):
    def tiled(x):
        return x.reshape(4, 4, 32, 128).transpose(0, 2, 1, 3).reshape(512, 128)

    anywhere = pl.BlockSpec(memory_space=pl.ANY)
    scalar = pl.BlockSpec(memory_space=pltpu.SMEM)
    forward, backward = pl.pallas_call(
        kernel,
        out_shape=[jax.ShapeDtypeStruct((2048, 128), F32)] * 2,
        in_specs=[anywhere] * 6 + [scalar] * 2,
        out_specs=[anywhere] * 2,
        scratch_shapes=[
            pltpu.VMEM((512, 128), F32),
            pltpu.VMEM((512, 128), F32),
            pltpu.VMEM((6, 4, 256, 256), F32),
            pltpu.VMEM((6, 4, 256, 256), F32),
            pltpu.VMEM((4, 4, 256, 256), F32),
            pltpu.VMEM((4, 4, 256, 256), F32),
            pltpu.VMEM((8, 64, 128), F32),
            pltpu.VMEM((8, 64, 128), F32),
            pltpu.VMEM((4, 64, 128), F32),
            pltpu.VMEM((3, 16, 64, 128), F32),
            pltpu.VMEM((3, 16, 64, 128), F32),
            pltpu.VMEM((16, 64, 128), F32),
            pltpu.VMEM((16, 64, 128), F32),
            pltpu.VMEM((16, 64, 128), F32),
            pltpu.VMEM((4, 8, 64, 128), F32),
            pltpu.VMEM((4, 8, 64, 128), F32),
        ]
        + [pltpu.VMEM((4, 256, 512), BF16)] * 7
        + [
            pltpu.VMEM((2048, 128), F32),
            pltpu.VMEM((2048, 128), F32),
            pltpu.SemaphoreType.DMA((PHASES,)),
            pltpu.SemaphoreType.DMA((PHASES,)),
            pltpu.SemaphoreType.DMA((12,)),
            pltpu.SemaphoreType.DMA((8,)),
        ],
        compiler_params=pltpu.CompilerParams(
            collective_id=0, has_side_effects=True, vmem_limit_bytes=58 * 1024 * 1024
        ),
    )(
        tiled(right_side), tiled(layer_sums[0]), lower_blocks, upper_blocks, lower_inverse,
        upper_diagonal_inverses, pattern.T, parents,
    )

    def untiled(x):
        return x.reshape(4, 128, 4, 128).transpose(0, 2, 1, 3).reshape(4, 4, 16384)

    return untiled(forward), untiled(backward)


def solution(mesh):
    in_specs = (
        P(None, "col", "row"),
        P("gz", None, "col", "row"),
        P(None, "col", "row", None),
        P(None, "col", "row", None),
        P(None, "col", None, None),
        P(None, "col", None, None),
        P(None, "col"),
        P(),
    )
    out_specs = (P(None, "col", None), P(None, "col", None))
    return jax.shard_map(body, mesh=mesh, in_specs=in_specs, out_specs=out_specs, check_vma=False)
```

time: 622 us -> 116 us (0.19); the launches traced: 612 us -> 116 us
  waiting for transfers between devices: 408 us -> 0 us
  Pallas kernels: 0 us -> 110 us
  blocking collectives: 88.9 us -> 0 us
  matrix products: 70.5 us -> 0 us
  local copies, waits for them, and re-layouts: 19.9 us -> 4.52 us
  between operations: 15 us -> 0.64 us
  other arithmetic: 9.55 us -> 0 us
    reduce_scatter x3 -> x0, waiting for transfers between devices: 240 us -> none  [body(): lax.psum_scatter(jnp.stack(summand_terms, 1), 'col', scatter_dimension=0,...]
    all_gather x3 -> x0, waiting for transfers between devices: 140 us -> none  [body(): whole_levels[height] = lax.all_gather(solved, 'col', axis=0, tiled=True)]
    pallas_call x0 -> x1, Pallas kernels: none -> 110 us  [body(): pl.pallas_call(kernel, out_shape=[jax.ShapeDtypeStruct((2048, 128), F32)]...]
    all_gather x8 -> x0, blocking collectives: 88.9 us -> none  [solve_nodes(): full_rows = lax.all_gather(pieces, 'row', axis=1, tiled=True)]
    dot_general x32 -> x0, matrix products: 70.5 us -> none  [the longest x6 35.1 us: body(): jnp.einsum('ja,awk->jwk', picker_masks[height, distance], whole_levels[he...]
    psum x1 -> x0, waiting for transfers between devices: 27.7 us -> none  [body(): lax.psum(layer_sums[0], 'gz').reshape(4, per_column, part_rows, COLUMNS)]
    another operation x11 -> x0, local copies, waits for them, and re-layouts: 15.1 us -> none  [the longest x3 13.2 us: body(): jnp.stack(summand_terms, 1)]
  transfers between devices with their start and end apart: 7 -> 0, of which waited for: 7 -> 0; matrix products, arithmetic and copies ran while one was open for 4% -> 0% of each run, Pallas kernels for 0% -> 0%
where the time goes in v2:
time: 116 us
  Pallas kernels  110 us (95%)
  local copies, waits for them, and re-layouts  4.52 us (4%)
    pallas_call x1, Pallas kernels, body(): pl.pallas_call(kernel, out_shape=[jax.ShapeDtypeStruct((2048, 128), F32)]...  110 us
    unnamed x2, local copies, waits for them, and re-layouts  4.52 us

profile of v2, /device:TPU:1, one launch (start us, length us, event | category | flops | bytes accessed | tf_op | source)
XLA Modules:
  0.0 115.6 jit_solution(7614155064218438596)
XLA Ops:
  0.6 110.4 %shard_map.95 = (f32[2048,128]{1,0:T(8,128)}, f32[2048,128]{1,0:T(8,128)}) custom-call(f32[512,128]{1,0:T(8,128)} %bitcast.23, f32[512,128]{1,0:T(8,128)} %bitcast.24, f32[6,4,64,256]{3,2,1,0:T(8,128)} %lower_hbm.1, f32[6,4,64,256]{3,2,1,0:T(8,128)} %upper_hbm.1, f32[4,4,256,256]{3,2,1,0:T(8,128)} %linv_hbm.1, f32[4,4,256,256]{3,2,1,0:T(8,128)} %uinv_hbm.1, ...), custom_call_target="tpu_custom_call" | custom-call | tf_op jit(solution)/shard_map/pallas_call | solution.py:437
  111.1 2.3 %copy.16 = f32[4,4,16384]{2,1,0:T(4,128)} copy(f32[4,4,16384]{2,1,0:T(4,128)} %bitcast.22) | data formatting | bytes 2097152
  113.3 2.3 %copy.17 = f32[4,4,16384]{2,1,0:T(4,128)} copy(f32[4,4,16384]{2,1,0:T(4,128)} %bitcast.21) | data formatting | bytes 2097152

commit v3 on v2

v3 whole, which is shorter than its diff:
```python
import jax
import jax.numpy as jnp
from jax import lax
from jax.experimental import pallas as pl
from jax.experimental.pallas import tpu as pltpu
from jax.sharding import PartitionSpec as P

MESH = pl.DeviceIdType.MESH
F32 = jnp.float32
BF16 = jnp.bfloat16
LANES = 128
PART = 64
NODES_HERE = 4
OFFSETS = sorted(
    [(dz, dy) for dz in range(4) for dy in range(4) if dz or dy],
    key=lambda o: -(min(o[0], 4 - o[0]) + min(o[1], 4 - o[1])),
)
INPUT, SCATTER, GATHER, RHS, F_GZ, Y_ROW, Y_GZ, PX = 0, 1, 4, 7, 11, 15, 19, 22
L_NEAR, L_FAR, L_GZ, U_NEAR, U_FAR, U_GZ, PHASES = 25, 28, 31, 34, 40, 46, 52


def place_of(height, distance):
    return height * (height - 1) // 2 + distance - 1


def lane_ids(rows):
    return lax.broadcasted_iota(jnp.int32, (rows, LANES), 1)


def split(x):
    high = x.astype(BF16)
    return high, (x - high.astype(F32)).astype(BF16)


def dot(a, b):
    return jnp.dot(a, b, preferred_element_type=F32)


def wide_of(a):
    return jnp.concatenate(split(a), axis=1)


def rolled(x, lanes):
    lanes = lanes % LANES
    return pltpu.roll(x, lanes, 1) if lanes else x


def operand_of(x):
    full = jnp.concatenate([rolled(x, -8 * part) for part in range(4)], axis=0)
    high = full.astype(BF16).astype(F32)
    low = full - high
    first = (lane_ids(256) // 8) % 4 == 0
    both = jnp.where(first, high, rolled(low.astype(BF16).astype(F32), 8))
    alone = jnp.where(first, high, 0.0)
    return jnp.concatenate([both.astype(BF16), alone.astype(BF16)], axis=0)


def apply(matrix_of, operand):
    node = lane_ids(256) // 32
    total = None
    for m in range(NODES_HERE):
        out = dot(matrix_of(m), operand)
        total = out if total is None else jnp.where(node == m, out, total)
    total = total + rolled(total, -8)
    quarter = (lane_ids(PART) // 8) % 4
    packed = None
    for part in range(4):
        moved = rolled(total[part * PART:(part + 1) * PART], 8 * part)
        packed = moved if packed is None else jnp.where(quarter == part, moved, packed)
    return packed


def pair_of(b):
    high, low = split(b)
    return high, jnp.concatenate([high, low], axis=1)


def product(a, b_pair):
    a_high, a_low = split(a)
    b_high, b_both = b_pair
    wide = dot(a_high, b_both)
    return wide[:, :LANES] + wide[:, LANES:] + dot(a_low, b_high)


def exchange(arrays):
    octet = lane_ids(arrays[0].shape[0]) // 8
    arrays = list(arrays)
    for bit in (1, 2, 4, 8)[: len(arrays).bit_length() - 1]:
        low = (octet // bit) % 2 == 0
        for i in range(len(arrays)):
            if i & bit:
                continue
            a, b = arrays[i], arrays[i | bit]
            arrays[i] = jnp.where(low, a, rolled(b, 8 * bit))
            arrays[i | bit] = jnp.where(low, rolled(a, -8 * bit), b)
    return arrays


def kernel(
    right_hbm, sums_hbm, lower_hbm, upper_hbm, linv_hbm, uinv_hbm, pattern_ref, parents_ref,
    fwd_hbm, bwd_hbm,
    right, sums, lower, lpart, upper, linv, uinv,
    xsend, xrecv, init, sbuf, qbuf, gbuf0, gbuf1, gbuf2, rbuf, pxsend, pxrecv,
    full, fbuf, fown, ybuf, vpart, top_inv, v21, v11, ul, w11, w21, w31, out_f, out_b,
    send_sem, recv_sem, load_sem, store_sem,
):
    g = lax.axis_index("gz")
    r = lax.axis_index("row")
    c = lax.axis_index("col")
    z, y = c // 4, c % 4
    me = g * 4 + r
    gbuf = (gbuf0, gbuf1, gbuf2)

    def column(offset):
        return ((z + offset[0]) % 4) * 4 + (y + offset[1]) % 4

    loads = {}

    def load(name, source, target):
        loads[name] = pltpu.make_async_copy(source, target, load_sem.at[len(loads)])
        loads[name].start()

    my_rows = pl.ds(pl.multiple_of(r * PART, PART), PART)
    my_nodes = pl.ds(g * 2, 2)
    load("right", right_hbm, right)
    load("sums", sums_hbm, sums)
    load("linv3", linv_hbm.at[3], linv.at[3])
    for height in (3, 2, 1):
        load(
            "lower%d" % height, lower_hbm.at[place_of(height, 1), my_nodes],
            lower.at[height - 1, my_nodes, my_rows, :],
        )
        for distance in range(2, height + 1):
            place = height + distance - 4
            load("lpart%d" % place, lower_hbm.at[place_of(height, distance)], lpart.at[place])
    load("linv2", linv_hbm.at[2], linv.at[2])
    load("linv1", linv_hbm.at[1], linv.at[1])
    load("upper", upper_hbm.at[:, my_nodes], upper.at[:, my_nodes, my_rows, :])
    load("linv0", linv_hbm.at[0], linv.at[0])
    for height in (0, 1, 2, 3):
        load("uinv%d" % height, uinv_hbm.at[height], uinv.at[height])

    barrier = pltpu.get_barrier_semaphore()
    for offset in OFFSETS:
        pl.semaphore_signal(
            barrier, inc=1, device_id={"col": column(offset)}, device_id_type=MESH
        )
    row_steps = (2, 1, 3)
    others = []
    for step in (2, 1, 3):
        others.append((g, (r + step) % 4))
        others.append((1 - g, (r + step) % 4))
    others.append((1 - g, r))
    for place in others:
        pl.semaphore_signal(
            barrier, inc=1, device_id={"gz": place[0], "row": place[1]}, device_id_type=MESH
        )

    def send(source, target, phase, place):
        pltpu.make_async_remote_copy(
            src_ref=source, dst_ref=target, send_sem=send_sem.at[phase],
            recv_sem=recv_sem.at[phase], device_id=place, device_id_type=MESH,
        ).start()

    def wait_bytes(whole, sem):
        pltpu.make_async_copy(whole, whole, sem).wait()

    def wait_blocks(sem, blocks):
        wait_bytes(qbuf.at[0, pl.ds(0, blocks)], sem)

    ancestor, stored = {}, {}
    for height in (1, 2, 3):
        for m in range(NODES_HERE):
            current = parents_ref[height - 1, c * NODES_HERE + m]
            for distance in range(1, height + 1):
                if distance > 1:
                    current = parents_ref[height - distance, current]
                ancestor[height, distance, m] = current
                stored[height, distance, m] = pattern_ref[m, place_of(height, distance)] != 0

    node_of = lane_ids(PART) // 32
    right_mate, left_mate = (r + 1) % 4, (r + 3) % 4

    def rows_of(part):
        return pl.ds(pl.multiple_of(part * PART, PART), PART)

    def near(source, q, target, at, phase):
        for mate in (right_mate, left_mate):
            send(
                source.at[q, my_nodes], target.at[at, my_nodes, my_rows, :], phase + at,
                {"row": mate},
            )

    def far(target, at, phase_near, phase_far):
        wait_bytes(upper.at[0, pl.ds(0, 2), pl.ds(0, 128), :], recv_sem.at[phase_near + at])
        for node, part, mate in ((2 * g, left_mate, right_mate), (2 * g + 1, right_mate, left_mate)):
            block = target.at[at, node, rows_of(part), :]
            send(block, block, phase_far + at, {"row": mate})

    def hand(target, at, phase_far, phase_gz):
        wait_bytes(upper.at[0, pl.ds(0, 2), pl.ds(0, 64), :], recv_sem.at[phase_far + at])
        send(target.at[at, my_nodes], target.at[at, my_nodes], phase_gz + at, {"gz": 1 - g})

    def l_near(height):
        near(lower_hbm, place_of(height, 1), lower, height - 1, L_NEAR)

    def l_far(height):
        far(lower, height - 1, L_NEAR, L_FAR)

    def l_hand(height):
        loads["lower%d" % height].wait()
        hand(lower, height - 1, L_FAR, L_GZ)

    def l_wait(height):
        wait_bytes(upper.at[0, pl.ds(0, 2)], recv_sem.at[L_GZ + height - 1])

    def u_near(q):
        near(upper_hbm, q, upper, q, U_NEAR)

    def u_far(q):
        far(upper, q, U_NEAR, U_FAR)

    def u_hand(q):
        hand(upper, q, U_FAR, U_GZ)

    def u_wait(q):
        wait_bytes(upper.at[0, pl.ds(0, 2)], recv_sem.at[U_GZ + q])

    def multiply(target, a_of, b_of):
        def one(m, carry):
            a_high, a_low = split(a_of(m))
            b_high, b_low = split(b_of(m))
            target[m] = wide_of(dot(a_high, b_high) + dot(a_high, b_low) + dot(a_low, b_high))
            return carry
        lax.fori_loop(0, NODES_HERE, one, 0)

    def scatter_terms(height, distance, terms_in, first, out):
        target = height - distance
        moved = {shift: rolled(terms_in, 32 * shift) for shift in range(-3, 4)}
        terms = []
        for m in range(NODES_HERE):
            spread = moved[-m]
            for t in range(1, 4):
                spread = jnp.where(node_of == t, moved[t - m], spread)
            terms.append(spread)
        wanted = [
            jnp.where(stored[height, distance, m], ancestor[height, distance, m], -1)
            for m in range(NODES_HERE)
        ]
        for offset in OFFSETS + [(0, 0)]:
            slot = offset[0] * 4 + offset[1]
            base = column(offset) * NODES_HERE
            total = jnp.zeros((PART, LANES), F32) if first else sbuf[target, slot]
            for m in range(NODES_HERE):
                total = total + jnp.where(node_of == wanted[m] - base, terms[m], 0.0)
            sbuf[target, slot] = total
            if out and slot:
                send(
                    sbuf.at[target, slot], qbuf.at[target, slot], SCATTER + target,
                    {"col": column(offset)},
                )

    def sum_received(target):
        wait_blocks(recv_sem.at[SCATTER + target], 15)
        total = init[target] - sbuf[target, 0]
        for slot in range(1, 16):
            total = total - qbuf[target, slot]
        return total

    def spread_rhs(height, value):
        rbuf[height, r] = value
        for step in row_steps:
            send(
                rbuf.at[height, r], rbuf.at[height, r], RHS + height, {"row": (r + step) % 4}
            )

    def take_rhs(height):
        wait_blocks(recv_sem.at[RHS + height], 3)
        blocks = exchange([rbuf[height, mate] for mate in range(4)])
        return pair_of(jnp.concatenate(blocks, axis=0))

    def make_vpart(height, distance):
        place = height + distance - 4
        q_rows = lpart.at[place]

        def one(m, carry):
            a_high, a_low = split(q_rows[m])
            b_high, b_low = split(linv[height, m])
            vpart[place, m] = dot(a_high, b_high) + dot(a_high, b_low) + dot(a_low, b_high)
            return carry

        lax.fori_loop(0, NODES_HERE, one, 0)

    def send_terms(height, distance, b_pair):
        place = height + distance - 4
        total = None
        for m in range(NODES_HERE):
            out = product(vpart[place, m], b_pair)
            total = out if total is None else jnp.where(node_of == m, out, total)
        pxrecv[place, r] = total
        for step in row_steps:
            moved = jnp.where(r + step < 4, rolled(total, -8 * step), rolled(total, 8 * (4 - step)))
            pxsend[place, step - 1] = moved
            send(
                pxsend.at[place, step - 1], pxrecv.at[place, r], PX + place,
                {"row": (r + step) % 4},
            )

    def take_terms(height, distance):
        place = height + distance - 4
        wait_blocks(recv_sem.at[PX + place], 3)
        quarter = (lane_ids(PART) // 8) % 4
        total = pxrecv[place, 0]
        for part in range(1, 4):
            total = jnp.where(quarter == part, pxrecv[place, part], total)
        return total

    def finish_forward(height, b_pair):
        node = lane_ids(256) // 32

        def one(m, carry):
            full[...] = jnp.where(node == m, product(linv[height, m], b_pair), full[...])
            return carry

        lax.fori_loop(0, NODES_HERE, one, 0)
        fbuf[height, g] = full[...]
        send(fbuf.at[height, g], fbuf.at[height, g], F_GZ + height, {"gz": 1 - g})
        if height:
            own = exchange([full[part * PART:(part + 1) * PART, :] for part in range(4)])
            for mate in range(4):
                fown[height - 1, mate] = own[mate]

    def write_forward(height, slot):
        wait_blocks(recv_sem.at[F_GZ + height], 4)
        group = lane_ids(128) // 32
        pieces = [
            fbuf[height, half, pl.ds(parity, 128, stride=2), :]
            for parity in range(2) for half in range(2)
        ]
        for m in range(NODES_HERE):
            total = None
            for place in range(4):
                moved = rolled(pieces[place], 32 * (place - m))
                total = moved if total is None else jnp.where(group == place, moved, total)
            out_f[pl.ds(height * 512 + m, 128, stride=4), :] = total
        rows = pl.ds(height * 512, 512)
        pltpu.make_async_copy(out_f.at[rows], fwd_hbm.at[rows], store_sem.at[slot]).start()

    my_octets = pl.ds(pl.multiple_of(g * 4, 4), 4)

    def spread_solution(height, value):
        ybuf[height, me] = value
        places = others if height == 3 else [(g, (r + step) % 4) for step in row_steps]
        for place in places:
            send(
                ybuf.at[height, me], ybuf.at[height, me], Y_ROW + height,
                {"gz": place[0], "row": place[1]},
            )

    def hand_solution(height):
        wait_blocks(recv_sem.at[Y_ROW + height], 3)
        send(ybuf.at[height, my_octets], ybuf.at[height, my_octets], Y_GZ + height, {"gz": 1 - g})

    def write_backward(height, slot):
        if height == 3:
            wait_blocks(recv_sem.at[Y_ROW + height], 7)
        else:
            wait_blocks(recv_sem.at[Y_GZ + height], 4)
        pieces = exchange([
            ybuf[height, octet, pl.ds(parity, 32, stride=2), :]
            for parity in range(2) for octet in range(8)
        ])
        for index in range(16):
            m, part = index // 4, index % 4
            out_b[pl.ds(height * 512 + part * 128 + m, 32, stride=4), :] = pieces[index]
        rows = pl.ds(height * 512, 512)
        pltpu.make_async_copy(out_b.at[rows], bwd_hbm.at[rows], store_sem.at[slot]).start()

    def chosen(height, distance):
        total = jnp.zeros((PART, LANES), F32)
        for m in range(NODES_HERE):
            a = ancestor[height, distance, m]
            chip = a // NODES_HERE
            slot = ((z + 4 - chip // 4) % 4) * 4 + (y + 4 - chip % 4) % 4
            block = gbuf[height - distance][slot]
            present = stored[height, distance, m]
            for source in range(4):
                here = jnp.where(jnp.logical_and(present, a % NODES_HERE == source), m, -1)
                total = jnp.where(node_of == here, rolled(block, 32 * (m - source)), total)
        return total

    def share_solution(height, value):
        gbuf[height][0] = value
        for offset in OFFSETS:
            slot = offset[0] * 4 + offset[1]
            send(
                gbuf[height].at[0], gbuf[height].at[slot], GATHER + height,
                {"col": column(offset)},
            )

    loads["right"].wait()
    loads["sums"].wait()
    sources = []
    for m in range(NODES_HERE):
        for height in range(4):
            rows = pl.ds(height * 128 + m, 32, stride=4)
            sources.append(jnp.where(g == 0, right[rows, :], 0.0) - sums[rows, :])
    pieces = exchange(sources)
    for parity in range(2):
        for octet in range(8):
            xsend[octet, pl.ds(parity, 32, stride=2), :] = pieces[parity * 8 + octet]
    pl.semaphore_wait(barrier, len(OFFSETS) + len(others))
    for place in others:
        send(
            xsend.at[place[0] * 4 + place[1]], xrecv.at[me], INPUT,
            {"gz": place[0], "row": place[1]},
        )
    l_near(3)
    xrecv[me] = xsend[me]
    loads["linv3"].wait()

    def widen_top(m, carry):
        top_inv[m] = wide_of(linv[3, m])
        return carry

    lax.fori_loop(0, NODES_HERE, widen_top, 0)
    loads["lpart1"].wait()
    make_vpart(3, 2)
    l_far(3)
    l_near(2)
    wait_blocks(recv_sem.at[INPUT], 7)
    parts = exchange([xrecv[part] + xrecv[4 + part] for part in range(4)])
    for height in range(4):
        init[height] = parts[height]

    spread_rhs(3, init[3])
    l_hand(3)
    operand = operand_of(apply(lambda m: top_inv[m], operand_of(init[3])))
    loads["lpart2"].wait()
    make_vpart(3, 3)
    l_wait(3)
    scatter_terms(3, 1, apply(lambda m: wide_of(lower[2, m]), operand), True, True)
    b_pair = take_rhs(3)
    send_terms(3, 2, b_pair)
    l_far(2)
    send_terms(3, 3, b_pair)
    l_near(1)
    finish_forward(3, b_pair)
    loads["linv2"].wait()
    loads["lpart0"].wait()
    make_vpart(2, 2)
    l_hand(2)
    l_wait(2)
    multiply(v21, lambda m: lower[1, m], lambda m: linv[2, m])
    l_far(1)
    scatter_terms(3, 2, take_terms(3, 2), True, False)

    rhs = sum_received(2)
    spread_rhs(2, rhs)
    scatter_terms(2, 1, apply(lambda m: v21[m], operand_of(rhs)), False, True)
    u_near(0)
    scatter_terms(3, 3, take_terms(3, 3), True, False)
    l_hand(1)
    b_pair = take_rhs(2)
    send_terms(2, 2, b_pair)
    finish_forward(2, b_pair)
    loads["linv1"].wait()
    l_wait(1)
    multiply(v11, lambda m: lower[0, m], lambda m: linv[1, m])
    u_far(0)
    u_near(2)
    scatter_terms(2, 2, take_terms(2, 2), False, False)

    rhs = sum_received(1)
    spread_rhs(1, rhs)
    scatter_terms(1, 1, apply(lambda m: v11[m], operand_of(rhs)), False, True)
    loads["upper"].wait()
    u_hand(0)
    u_far(2)
    u_near(1)
    finish_forward(1, take_rhs(1))
    loads["linv0"].wait()
    loads["uinv0"].wait()
    multiply(ul, lambda m: uinv[0, m], lambda m: linv[0, m])
    loads["uinv1"].wait()
    rest1 = apply(lambda m: wide_of(uinv[1, m]), operand_of(fown[0, r]))
    u_hand(2)
    u_far(1)
    u_near(5)
    u_wait(0)
    multiply(w11, lambda m: uinv[1, m], lambda m: upper[0, m])

    rhs = sum_received(0)
    value = apply(lambda m: ul[m], operand_of(rhs))
    share_solution(0, value)
    spread_rhs(0, rhs)
    spread_solution(0, value)
    u_hand(1)
    u_far(5)
    u_near(4)
    finish_forward(0, take_rhs(0))
    hand_solution(0)
    u_wait(1)
    loads["uinv2"].wait()
    multiply(w21, lambda m: uinv[2, m], lambda m: upper[1, m])
    write_forward(3, 0)

    wait_blocks(recv_sem.at[GATHER + 0], 15)
    value = rest1 - apply(lambda m: w11[m], operand_of(chosen(1, 1)))
    share_solution(1, value)
    u_far(4)
    u_near(3)
    spread_solution(1, value)
    u_wait(2)
    rest = fown[1, r] - apply(lambda m: wide_of(upper[2, m]), operand_of(chosen(2, 2)))
    rest2 = apply(lambda m: wide_of(uinv[2, m]), operand_of(rest))
    u_hand(5)
    u_hand(4)
    u_far(3)
    write_forward(2, 1)
    hand_solution(1)

    wait_blocks(recv_sem.at[GATHER + 1], 15)
    value = rest2 - apply(lambda m: w21[m], operand_of(chosen(2, 1)))
    share_solution(2, value)
    spread_solution(2, value)
    u_hand(3)
    u_wait(5)
    rest = fown[2, r] - apply(lambda m: wide_of(upper[5, m]), operand_of(chosen(3, 3)))
    u_wait(4)
    rest = rest - apply(lambda m: wide_of(upper[4, m]), operand_of(chosen(3, 2)))
    loads["uinv3"].wait()
    rest3 = apply(lambda m: wide_of(uinv[3, m]), operand_of(rest))
    u_wait(3)
    multiply(w31, lambda m: uinv[3, m], lambda m: upper[3, m])
    hand_solution(2)

    wait_blocks(recv_sem.at[GATHER + 2], 15)
    value = rest3 - apply(lambda m: w31[m], operand_of(chosen(3, 1)))
    spread_solution(3, value)
    write_forward(1, 2)
    write_forward(0, 3)
    write_backward(0, 4)
    write_backward(1, 5)
    write_backward(2, 6)
    write_backward(3, 7)

    for phase, blocks in (
        [(INPUT, 7)]
        + [(SCATTER + t, 15) for t in range(3)]
        + [(GATHER + t, 15) for t in range(3)]
        + [(RHS + h, 3) for h in range(4)]
        + [(F_GZ + h, 4) for h in range(4)]
        + [(Y_ROW + h, 7 if h == 3 else 3) for h in range(4)]
        + [(Y_GZ + h, 4) for h in range(3)]
        + [(PX + p, 3) for p in range(3)]
        + [(L_NEAR + p, 8) for p in range(3)]
        + [(L_FAR + p, 4) for p in range(3)]
        + [(L_GZ + p, 16) for p in range(3)]
        + [(U_NEAR + p, 8) for p in range(6)]
        + [(U_FAR + p, 4) for p in range(6)]
        + [(U_GZ + p, 16) for p in range(6)]
    ):
        wait_blocks(send_sem.at[phase], blocks)
    for slot, (height, out, hbm) in enumerate(
        [(h, out_f, fwd_hbm) for h in (3, 2, 1, 0)] + [(h, out_b, bwd_hbm) for h in (0, 1, 2, 3)]
    ):
        rows = pl.ds(height * 512, 512)
        pltpu.make_async_copy(out.at[rows], hbm.at[rows], store_sem.at[slot]).wait()


def body(
    right_side, layer_sums, lower_blocks, upper_blocks, lower_inverse, upper_diagonal_inverses,
    pattern, parents,
):
    def tiled(x):
        return x.reshape(4, 4, 32, 128).transpose(0, 2, 1, 3).reshape(512, 128)

    anywhere = pl.BlockSpec(memory_space=pl.ANY)
    scalar = pl.BlockSpec(memory_space=pltpu.SMEM)
    forward, backward = pl.pallas_call(
        kernel,
        out_shape=[jax.ShapeDtypeStruct((2048, 128), F32)] * 2,
        in_specs=[anywhere] * 6 + [scalar] * 2,
        out_specs=[anywhere] * 2,
        scratch_shapes=[
            pltpu.VMEM((512, 128), F32),
            pltpu.VMEM((512, 128), F32),
            pltpu.VMEM((3, 4, 256, 256), F32),
            pltpu.VMEM((3, 4, 64, 256), F32),
            pltpu.VMEM((6, 4, 256, 256), F32),
            pltpu.VMEM((4, 4, 256, 256), F32),
            pltpu.VMEM((4, 4, 256, 256), F32),
            pltpu.VMEM((8, 64, 128), F32),
            pltpu.VMEM((8, 64, 128), F32),
            pltpu.VMEM((4, 64, 128), F32),
            pltpu.VMEM((3, 16, 64, 128), F32),
            pltpu.VMEM((3, 16, 64, 128), F32),
            pltpu.VMEM((16, 64, 128), F32),
            pltpu.VMEM((16, 64, 128), F32),
            pltpu.VMEM((16, 64, 128), F32),
            pltpu.VMEM((4, 4, 64, 128), F32),
            pltpu.VMEM((3, 3, 64, 128), F32),
            pltpu.VMEM((3, 4, 64, 128), F32),
            pltpu.VMEM((256, 128), F32),
            pltpu.VMEM((4, 2, 256, 128), F32),
            pltpu.VMEM((3, 4, 64, 128), F32),
            pltpu.VMEM((4, 8, 64, 128), F32),
            pltpu.VMEM((3, 4, 64, 256), F32),
        ]
        + [pltpu.VMEM((4, 256, 512), BF16)] * 7
        + [
            pltpu.VMEM((2048, 128), F32),
            pltpu.VMEM((2048, 128), F32),
            pltpu.SemaphoreType.DMA((PHASES,)),
            pltpu.SemaphoreType.DMA((PHASES,)),
            pltpu.SemaphoreType.DMA((20,)),
            pltpu.SemaphoreType.DMA((8,)),
        ],
        compiler_params=pltpu.CompilerParams(
            collective_id=0, has_side_effects=True, vmem_limit_bytes=58 * 1024 * 1024
        ),
    )(
        tiled(right_side), tiled(layer_sums[0]), lower_blocks, upper_blocks, lower_inverse,
        upper_diagonal_inverses, pattern.T, parents,
    )

    def untiled(x):
        return x.reshape(4, 128, 4, 128).transpose(0, 2, 1, 3).reshape(4, 4, 16384)

    return untiled(forward), untiled(backward)


def solution(mesh):
    in_specs = (
        P(None, "col", "row"),
        P("gz", None, "col", "row"),
        P(None, "col", "row", None),
        P(None, "col", "row", None),
        P(None, "col", None, None),
        P(None, "col", None, None),
        P(None, "col"),
        P(),
    )
    out_specs = (P(None, "col", None), P(None, "col", None))
    return jax.shard_map(body, mesh=mesh, in_specs=in_specs, out_specs=out_specs, check_vma=False)
```

time: 116 us -> 94.9 us (0.82)
  Pallas kernels: 110 us -> 89.5 us
    pallas_call x1, Pallas kernels: 110 us -> 89.5 us  [body(): pl.pallas_call(kernel, out_shape=[jax.ShapeDtypeStruct((2048, 128), F32)]...]
where the time goes in v3:
time: 94.9 us; the launch traced here: 94.7 us
  Pallas kernels  89.5 us (94%)
  local copies, waits for them, and re-layouts  4.52 us (5%)
    pallas_call x1, Pallas kernels, body(): pl.pallas_call(kernel, out_shape=[jax.ShapeDtypeStruct((2048, 128), F32)]...  89.5 us
    unnamed x2, local copies, waits for them, and re-layouts  4.52 us

profile of v3, /device:TPU:1, one launch (start us, length us, event | category | flops | bytes accessed | tf_op | source)
XLA Modules:
  0.0 94.7 jit_solution(18327752362331245230)
XLA Ops:
  0.6 89.5 %shard_map.95 = (f32[2048,128]{1,0:T(8,128)}, f32[2048,128]{1,0:T(8,128)}) custom-call(f32[512,128]{1,0:T(8,128)} %bitcast.23, f32[512,128]{1,0:T(8,128)} %bitcast.24, f32[6,4,64,256]{3,2,1,0:T(8,128)} %lower_hbm.1, f32[6,4,64,256]{3,2,1,0:T(8,128)} %upper_hbm.1, f32[4,4,256,256]{3,2,1,0:T(8,128)} %linv_hbm.1, f32[4,4,256,256]{3,2,1,0:T(8,128)} %uinv_hbm.1, ...), custom_call_target="tpu_custom_call" | custom-call | tf_op jit(solution)/shard_map/pallas_call | solution.py:581
  90.1 2.3 %copy.16 = f32[4,4,16384]{2,1,0:T(4,128)} copy(f32[4,4,16384]{2,1,0:T(4,128)} %bitcast.22) | data formatting | bytes 2097152
  92.4 2.3 %copy.17 = f32[4,4,16384]{2,1,0:T(4,128)} copy(f32[4,4,16384]{2,1,0:T(4,128)} %bitcast.21) | data formatting | bytes 2097152

commit v4 on v3

--- a/solution.py
+++ b/solution.py
@@ -16,7 +16,7 @@
     key=lambda o: -(min(o[0], 4 - o[0]) + min(o[1], 4 - o[1])),
 )
 INPUT, SCATTER, GATHER, RHS, F_GZ, Y_ROW, Y_GZ, PX = 0, 1, 4, 7, 11, 15, 19, 22
-L_NEAR, L_FAR, L_GZ, U_NEAR, U_FAR, U_GZ, PHASES = 25, 28, 31, 34, 40, 46, 52
+L_NEAR, L_FAR, L_GZ, U_NEAR, U_FAR, U_GZ, TOP_IN, NEXT_IN, PHASES = 25, 28, 31, 34, 40, 46, 52, 53, 54
 
 
 def place_of(height, distance):
@@ -100,8 +100,8 @@
     right_hbm, sums_hbm, lower_hbm, upper_hbm, linv_hbm, uinv_hbm, pattern_ref, parents_ref,
     fwd_hbm, bwd_hbm,
     right, sums, lower, lpart, upper, linv, uinv,
-    xsend, xrecv, init, sbuf, qbuf, gbuf0, gbuf1, gbuf2, rbuf, pxsend, pxrecv,
-    full, fbuf, fown, ybuf, vpart, top_inv, v21, v11, ul, w11, w21, w31, out_f, out_b,
+    topsend, toprecv, nextsend, nextrecv, xsend, xrecv, init, sbuf, qbuf, gbuf0, gbuf1, gbuf2, rbuf, pxsend, pxrecv,
+    full, fbuf, fown, ybuf, vpart, ownrhs, v21, v11, ul, w11, w21, w31, out_f, out_b,
     send_sem, recv_sem, load_sem, store_sem,
 ):
     g = lax.axis_index("gz")
@@ -126,10 +126,13 @@
     load("sums", sums_hbm, sums)
     load("linv3", linv_hbm.at[3], linv.at[3])
     for height in (3, 2, 1):
-        load(
-            "lower%d" % height, lower_hbm.at[place_of(height, 1), my_nodes],
-            lower.at[height - 1, my_nodes, my_rows, :],
-        )
+        if height < 3:
+            load(
+                "lower%d" % height, lower_hbm.at[place_of(height, 1), my_nodes],
+                lower.at[height - 1, my_nodes, my_rows, :],
+            )
+        else:
+            load("lpart3", lower_hbm.at[place_of(3, 1)], lpart.at[3])
         for distance in range(2, height + 1):
             place = height + distance - 4
             load("lpart%d" % place, lower_hbm.at[place_of(height, distance)], lpart.at[place])
@@ -276,11 +279,17 @@
 
     def take_rhs(height):
         wait_blocks(recv_sem.at[RHS + height], 3)
-        blocks = exchange([rbuf[height, mate] for mate in range(4)])
+        blocks = [rbuf[height, mate] for mate in range(4)]
+        if height == 2:
+            own = exchange(blocks)
+            for mate in range(4):
+                ownrhs[mate] = own[mate]
+        else:
+            blocks = exchange(blocks)
         return pair_of(jnp.concatenate(blocks, axis=0))
 
     def make_vpart(height, distance):
-        place = height + distance - 4
+        place = 3 if distance == 1 else height + distance - 4
         q_rows = lpart.at[place]
 
         def one(m, carry):
@@ -291,12 +300,16 @@
 
         lax.fori_loop(0, NODES_HERE, one, 0)
 
-    def send_terms(height, distance, b_pair):
-        place = height + distance - 4
+    def part_terms(place, b_pair):
         total = None
         for m in range(NODES_HERE):
             out = product(vpart[place, m], b_pair)
             total = out if total is None else jnp.where(node_of == m, out, total)
+        return total
+
+    def send_terms(height, distance, b_pair):
+        place = height + distance - 4
+        total = part_terms(place, b_pair)
         pxrecv[place, r] = total
         for step in row_steps:
             moved = jnp.where(r + step < 4, rolled(total, -8 * step), rolled(total, 8 * (4 - step)))
@@ -400,69 +413,87 @@
 
     loads["right"].wait()
     loads["sums"].wait()
-    sources = []
-    for m in range(NODES_HERE):
-        for height in range(4):
-            rows = pl.ds(height * 128 + m, 32, stride=4)
-            sources.append(jnp.where(g == 0, right[rows, :], 0.0) - sums[rows, :])
-    pieces = exchange(sources)
+
+    def source_of(height, m):
+        rows = pl.ds(height * 128 + m, 32, stride=4)
+        return jnp.where(g == 0, right[rows, :], 0.0) - sums[rows, :]
+
+    group32 = lane_ids(32) // 32
+
+    def half_of(blocks, parity, half):
+        total = None
+        for m in range(NODES_HERE):
+            moved = rolled(blocks[m], 32 * (m - 2 * parity - half))
+            total = moved if total is None else jnp.where(group32 == m, moved, total)
+        return total
+
+    for height in (3, 2):
+        blocks = [source_of(height, m) for m in range(NODES_HERE)]
+        for parity in range(2):
+            rows = pl.ds(parity, 32, stride=2)
+            halves = [half_of(blocks, parity, half) for half in range(2)]
+            if height == 3:
+                topsend[0, rows, :] = halves[0]
+                topsend[1, rows, :] = halves[1]
+            else:
+                init[2, rows, :] = jnp.where(g == 0, halves[0], halves[1])
+                nextsend[rows, :] = jnp.where(g == 0, halves[1], halves[0])
+    toprecv[me] = topsend[g]
+    pl.semaphore_wait(barrier, len(OFFSETS) + len(others))
+    for place in others:
+        send(
+            topsend.at[place[0]], toprecv.at[me], TOP_IN, {"gz": place[0], "row": place[1]},
+        )
+    send(nextsend, nextrecv, NEXT_IN, {"gz": 1 - g})
+    l_near(2)
+    loads["linv3"].wait()
+    loads["lpart3"].wait()
+    make_vpart(3, 1)
+    loads["lpart1"].wait()
+    make_vpart(3, 2)
+    wait_blocks(recv_sem.at[TOP_IN], 7)
+
+    b_pair = pair_of(jnp.concatenate([toprecv[part] + toprecv[4 + part] for part in range(4)], axis=0))
+    scatter_terms(3, 1, part_terms(3, b_pair), True, True)
+    send_terms(3, 2, b_pair)
+    l_far(2)
+    loads["lpart2"].wait()
+    make_vpart(3, 3)
+    send_terms(3, 3, b_pair)
+    pieces = exchange([source_of(height, m) for m in range(NODES_HERE) for height in range(4)])
     for parity in range(2):
         for octet in range(8):
             xsend[octet, pl.ds(parity, 32, stride=2), :] = pieces[parity * 8 + octet]
-    pl.semaphore_wait(barrier, len(OFFSETS) + len(others))
     for place in others:
         send(
             xsend.at[place[0] * 4 + place[1]], xrecv.at[me], INPUT,
             {"gz": place[0], "row": place[1]},
         )
-    l_near(3)
     xrecv[me] = xsend[me]
-    loads["linv3"].wait()
-
-    def widen_top(m, carry):
-        top_inv[m] = wide_of(linv[3, m])
-        return carry
-
-    lax.fori_loop(0, NODES_HERE, widen_top, 0)
-    loads["lpart1"].wait()
-    make_vpart(3, 2)
-    l_far(3)
-    l_near(2)
-    wait_blocks(recv_sem.at[INPUT], 7)
-    parts = exchange([xrecv[part] + xrecv[4 + part] for part in range(4)])
-    for height in range(4):
-        init[height] = parts[height]
-
-    spread_rhs(3, init[3])
-    l_hand(3)
-    operand = operand_of(apply(lambda m: top_inv[m], operand_of(init[3])))
-    loads["lpart2"].wait()
-    make_vpart(3, 3)
-    l_wait(3)
-    scatter_terms(3, 1, apply(lambda m: wide_of(lower[2, m]), operand), True, True)
-    b_pair = take_rhs(3)
-    send_terms(3, 2, b_pair)
-    l_far(2)
-    send_terms(3, 3, b_pair)
     l_near(1)
+    l_hand(2)
     finish_forward(3, b_pair)
     loads["linv2"].wait()
     loads["lpart0"].wait()
     make_vpart(2, 2)
-    l_hand(2)
+    wait_blocks(recv_sem.at[NEXT_IN], 1)
+    init[2] = init[2] + nextrecv[...]
     l_wait(2)
     multiply(v21, lambda m: lower[1, m], lambda m: linv[2, m])
+    scatter_terms(3, 2, take_terms(3, 2), True, False)
+
+    spread_rhs(2, sum_received(2))
     l_far(1)
-    scatter_terms(3, 2, take_terms(3, 2), True, False)
-
-    rhs = sum_received(2)
-    spread_rhs(2, rhs)
-    scatter_terms(2, 1, apply(lambda m: v21[m], operand_of(rhs)), False, True)
+    scatter_terms(3, 3, take_terms(3, 3), True, False)
+    wait_blocks(recv_sem.at[INPUT], 7)
+    parts = exchange([xrecv[part] + xrecv[4 + part] for part in range(4)])
+    for height in range(2):
+        init[height] = parts[height]
+    b_pair = take_rhs(2)
+    scatter_terms(2, 1, apply(lambda m: v21[m], operand_of(ownrhs[r])), False, True)
+    send_terms(2, 2, b_pair)
     u_near(0)
-    scatter_terms(3, 3, take_terms(3, 3), True, False)
     l_hand(1)
-    b_pair = take_rhs(2)
-    send_terms(2, 2, b_pair)
     finish_forward(2, b_pair)
     loads["linv1"].wait()
     l_wait(1)
@@ -546,17 +577,17 @@
     write_backward(3, 7)
 
     for phase, blocks in (
-        [(INPUT, 7)]
+        [(INPUT, 7), (TOP_IN, 7), (NEXT_IN, 1)]
         + [(SCATTER + t, 15) for t in range(3)]
         + [(GATHER + t, 15) for t in range(3)]
-        + [(RHS + h, 3) for h in range(4)]
+        + [(RHS + h, 3) for h in range(3)]
         + [(F_GZ + h, 4) for h in range(4)]
         + [(Y_ROW + h, 7 if h == 3 else 3) for h in range(4)]
         + [(Y_GZ + h, 4) for h in range(3)]
         + [(PX + p, 3) for p in range(3)]
-        + [(L_NEAR + p, 8) for p in range(3)]
-        + [(L_FAR + p, 4) for p in range(3)]
-        + [(L_GZ + p, 16) for p in range(3)]
+        + [(L_NEAR + p, 8) for p in range(2)]
+        + [(L_FAR + p, 4) for p in range(2)]
+        + [(L_GZ + p, 16) for p in range(2)]
         + [(U_NEAR + p, 8) for p in range(6)]
         + [(U_FAR + p, 4) for p in range(6)]
         + [(U_GZ + p, 16) for p in range(6)]
@@ -586,11 +617,15 @@
         scratch_shapes=[
             pltpu.VMEM((512, 128), F32),
             pltpu.VMEM((512, 128), F32),
-            pltpu.VMEM((3, 4, 256, 256), F32),
-            pltpu.VMEM((3, 4, 64, 256), F32),
+            pltpu.VMEM((2, 4, 256, 256), F32),
+            pltpu.VMEM((4, 4, 64, 256), F32),
             pltpu.VMEM((6, 4, 256, 256), F32),
             pltpu.VMEM((4, 4, 256, 256), F32),
             pltpu.VMEM((4, 4, 256, 256), F32),
+            pltpu.VMEM((2, 64, 128), F32),
+            pltpu.VMEM((8, 64, 128), F32),
+            pltpu.VMEM((64, 128), F32),
+            pltpu.VMEM((64, 128), F32),
             pltpu.VMEM((8, 64, 128), F32),
             pltpu.VMEM((8, 64, 128), F32),
             pltpu.VMEM((4, 64, 128), F32),
@@ -599,16 +634,17 @@
             pltpu.VMEM((16, 64, 128), F32),
             pltpu.VMEM((16, 64, 128), F32),
             pltpu.VMEM((16, 64, 128), F32),
-            pltpu.VMEM((4, 4, 64, 128), F32),
+            pltpu.VMEM((3, 4, 64, 128), F32),
             pltpu.VMEM((3, 3, 64, 128), F32),
             pltpu.VMEM((3, 4, 64, 128), F32),
             pltpu.VMEM((256, 128), F32),
             pltpu.VMEM((4, 2, 256, 128), F32),
             pltpu.VMEM((3, 4, 64, 128), F32),
             pltpu.VMEM((4, 8, 64, 128), F32),
-            pltpu.VMEM((3, 4, 64, 256), F32),
+            pltpu.VMEM((4, 4, 64, 256), F32),
+            pltpu.VMEM((4, 64, 128), F32),
         ]
-        + [pltpu.VMEM((4, 256, 512), BF16)] * 7
+        + [pltpu.VMEM((4, 256, 512), BF16)] * 6
         + [
             pltpu.VMEM((2048, 128), F32),
             pltpu.VMEM((2048, 128), F32),

time: 94.9 us -> 88.9 us (0.937)
  Pallas kernels: 89.5 us -> 83.5 us
    pallas_call x1, Pallas kernels: 89.5 us -> 83.5 us  [body(): pl.pallas_call(kernel, out_shape=[jax.ShapeDtypeStruct((2048, 128), F32)]...]
where the time goes in v4:
time: 88.9 us; the launch traced here: 88.7 us
  Pallas kernels  83.5 us (94%)
  local copies, waits for them, and re-layouts  4.52 us (5%)
    pallas_call x1, Pallas kernels, body(): pl.pallas_call(kernel, out_shape=[jax.ShapeDtypeStruct((2048, 128), F32)]...  83.5 us
    unnamed x2, local copies, waits for them, and re-layouts  4.52 us

profile of v4, /device:TPU:1, one launch (start us, length us, event | category | flops | bytes accessed | tf_op | source)
XLA Modules:
  0.0 88.7 jit_solution(11854570868564247603)
XLA Ops:
  0.6 83.5 %shard_map.95 = (f32[2048,128]{1,0:T(8,128)}, f32[2048,128]{1,0:T(8,128)}) custom-call(f32[512,128]{1,0:T(8,128)} %bitcast.23, f32[512,128]{1,0:T(8,128)} %bitcast.24, f32[6,4,64,256]{3,2,1,0:T(8,128)} %lower_hbm.1, f32[6,4,64,256]{3,2,1,0:T(8,128)} %upper_hbm.1, f32[4,4,256,256]{3,2,1,0:T(8,128)} %linv_hbm.1, f32[4,4,256,256]{3,2,1,0:T(8,128)} %uinv_hbm.1, ...), custom_call_target="tpu_custom_call" | custom-call | tf_op jit(solution)/shard_map/pallas_call | solution.py:612
  84.1 2.3 %copy.16 = f32[4,4,16384]{2,1,0:T(4,128)} copy(f32[4,4,16384]{2,1,0:T(4,128)} %bitcast.22) | data formatting | bytes 2097152
  86.4 2.3 %copy.17 = f32[4,4,16384]{2,1,0:T(4,128)} copy(f32[4,4,16384]{2,1,0:T(4,128)} %bitcast.21) | data formatting | bytes 2097152

commit v5 on v4

--- a/solution.py
+++ b/solution.py
@@ -310,23 +310,18 @@
     def send_terms(height, distance, b_pair):
         place = height + distance - 4
         total = part_terms(place, b_pair)
-        pxrecv[place, r] = total
+        blocks = exchange([total[16 * part:16 * part + 16] for part in range(4)])
+        for mate in range(4):
+            pxsend[place, mate] = blocks[mate]
+        pxrecv[place, r] = pxsend[place, r]
         for step in row_steps:
-            moved = jnp.where(r + step < 4, rolled(total, -8 * step), rolled(total, 8 * (4 - step)))
-            pxsend[place, step - 1] = moved
-            send(
-                pxsend.at[place, step - 1], pxrecv.at[place, r], PX + place,
-                {"row": (r + step) % 4},
-            )
+            to = (r + step) % 4
+            send(pxsend.at[place, to], pxrecv.at[place, r], PX + place, {"row": to})
 
     def take_terms(height, distance):
         place = height + distance - 4
-        wait_blocks(recv_sem.at[PX + place], 3)
-        quarter = (lane_ids(PART) // 8) % 4
-        total = pxrecv[place, 0]
-        for part in range(1, 4):
-            total = jnp.where(quarter == part, pxrecv[place, part], total)
-        return total
+        wait_bytes(pxrecv.at[place, pl.ds(0, 3)], recv_sem.at[PX + place])
+        return jnp.concatenate(exchange([pxrecv[place, mate] for mate in range(4)]), axis=0)
 
     def finish_forward(height, b_pair):
         node = lane_ids(256) // 32
@@ -460,10 +455,9 @@
     loads["lpart2"].wait()
     make_vpart(3, 3)
     send_terms(3, 3, b_pair)
-    pieces = exchange([source_of(height, m) for m in range(NODES_HERE) for height in range(4)])
-    for parity in range(2):
-        for octet in range(8):
-            xsend[octet, pl.ds(parity, 32, stride=2), :] = pieces[parity * 8 + octet]
+    pieces = exchange([source_of(height, m) for height in range(2) for m in range(NODES_HERE)])
+    for octet in range(8):
+        xsend[octet] = pieces[octet]
     for place in others:
         send(
             xsend.at[place[0] * 4 + place[1]], xrecv.at[me], INPUT,
@@ -471,8 +465,9 @@
         )
     xrecv[me] = xsend[me]
     l_near(1)
+    u_near(0)
+    finish_forward(3, b_pair)
     l_hand(2)
-    finish_forward(3, b_pair)
     loads["linv2"].wait()
     loads["lpart0"].wait()
     make_vpart(2, 2)
@@ -485,21 +480,22 @@
     spread_rhs(2, sum_received(2))
     l_far(1)
     scatter_terms(3, 3, take_terms(3, 3), True, False)
-    wait_blocks(recv_sem.at[INPUT], 7)
+    wait_bytes(xrecv.at[pl.ds(0, 7)], recv_sem.at[INPUT])
     parts = exchange([xrecv[part] + xrecv[4 + part] for part in range(4)])
     for height in range(2):
-        init[height] = parts[height]
+        for parity in range(2):
+            init[height, pl.ds(parity, 32, stride=2), :] = half_of(parts, parity, height)
     b_pair = take_rhs(2)
     scatter_terms(2, 1, apply(lambda m: v21[m], operand_of(ownrhs[r])), False, True)
     send_terms(2, 2, b_pair)
-    u_near(0)
+    u_far(0)
+    u_near(2)
     l_hand(1)
+    u_near(1)
     finish_forward(2, b_pair)
     loads["linv1"].wait()
     l_wait(1)
     multiply(v11, lambda m: lower[0, m], lambda m: linv[1, m])
-    u_far(0)
-    u_near(2)
     scatter_terms(2, 2, take_terms(2, 2), False, False)
 
     rhs = sum_received(1)
@@ -508,16 +504,15 @@
     loads["upper"].wait()
     u_hand(0)
     u_far(2)
-    u_near(1)
+    u_far(1)
+    u_near(5)
     finish_forward(1, take_rhs(1))
+    u_near(4)
     loads["linv0"].wait()
     loads["uinv0"].wait()
     multiply(ul, lambda m: uinv[0, m], lambda m: linv[0, m])
     loads["uinv1"].wait()
     rest1 = apply(lambda m: wide_of(uinv[1, m]), operand_of(fown[0, r]))
-    u_hand(2)
-    u_far(1)
-    u_near(5)
     u_wait(0)
     multiply(w11, lambda m: uinv[1, m], lambda m: upper[0, m])
 
@@ -527,9 +522,11 @@
     spread_rhs(0, rhs)
     spread_solution(0, value)
     u_hand(1)
+    u_hand(2)
     u_far(5)
-    u_near(4)
+    u_far(4)
     finish_forward(0, take_rhs(0))
+    u_near(3)
     hand_solution(0)
     u_wait(1)
     loads["uinv2"].wait()
@@ -539,15 +536,13 @@
     wait_blocks(recv_sem.at[GATHER + 0], 15)
     value = rest1 - apply(lambda m: w11[m], operand_of(chosen(1, 1)))
     share_solution(1, value)
-    u_far(4)
-    u_near(3)
     spread_solution(1, value)
+    u_hand(5)
+    u_hand(4)
+    u_far(3)
     u_wait(2)
     rest = fown[1, r] - apply(lambda m: wide_of(upper[2, m]), operand_of(chosen(2, 2)))
     rest2 = apply(lambda m: wide_of(uinv[2, m]), operand_of(rest))
-    u_hand(5)
-    u_hand(4)
-    u_far(3)
     write_forward(2, 1)
     hand_solution(1)
 
@@ -577,14 +572,13 @@
     write_backward(3, 7)
 
     for phase, blocks in (
-        [(INPUT, 7), (TOP_IN, 7), (NEXT_IN, 1)]
+        [(TOP_IN, 7), (NEXT_IN, 1)]
         + [(SCATTER + t, 15) for t in range(3)]
         + [(GATHER + t, 15) for t in range(3)]
         + [(RHS + h, 3) for h in range(3)]
         + [(F_GZ + h, 4) for h in range(4)]
         + [(Y_ROW + h, 7 if h == 3 else 3) for h in range(4)]
         + [(Y_GZ + h, 4) for h in range(3)]
-        + [(PX + p, 3) for p in range(3)]
         + [(L_NEAR + p, 8) for p in range(2)]
         + [(L_FAR + p, 4) for p in range(2)]
         + [(L_GZ + p, 16) for p in range(2)]
@@ -593,6 +587,9 @@
         + [(U_GZ + p, 16) for p in range(6)]
     ):
         wait_blocks(send_sem.at[phase], blocks)
+    wait_bytes(xrecv.at[pl.ds(0, 7)], send_sem.at[INPUT])
+    for place in range(3):
+        wait_bytes(pxrecv.at[place, pl.ds(0, 3)], send_sem.at[PX + place])
     for slot, (height, out, hbm) in enumerate(
         [(h, out_f, fwd_hbm) for h in (3, 2, 1, 0)] + [(h, out_b, bwd_hbm) for h in (0, 1, 2, 3)]
     ):
@@ -626,8 +623,8 @@
             pltpu.VMEM((8, 64, 128), F32),
             pltpu.VMEM((64, 128), F32),
             pltpu.VMEM((64, 128), F32),
-            pltpu.VMEM((8, 64, 128), F32),
-            pltpu.VMEM((8, 64, 128), F32),
+            pltpu.VMEM((8, 32, 128), F32),
+            pltpu.VMEM((8, 32, 128), F32),
             pltpu.VMEM((4, 64, 128), F32),
             pltpu.VMEM((3, 16, 64, 128), F32),
             pltpu.VMEM((3, 16, 64, 128), F32),
@@ -635,8 +632,8 @@
             pltpu.VMEM((16, 64, 128), F32),
             pltpu.VMEM((16, 64, 128), F32),
             pltpu.VMEM((3, 4, 64, 128), F32),
-            pltpu.VMEM((3, 3, 64, 128), F32),
-            pltpu.VMEM((3, 4, 64, 128), F32),
+            pltpu.VMEM((3, 4, 16, 128), F32),
+            pltpu.VMEM((3, 4, 16, 128), F32),
             pltpu.VMEM((256, 128), F32),
             pltpu.VMEM((4, 2, 256, 128), F32),
             pltpu.VMEM((3, 4, 64, 128), F32),

time: 88.9 us -> 85.1 us (0.957)
  Pallas kernels: 83.5 us -> 79.8 us
    pallas_call x1, Pallas kernels: 83.5 us -> 79.8 us  [body(): pl.pallas_call(kernel, out_shape=[jax.ShapeDtypeStruct((2048, 128), F32)]...]
where the time goes in v5:
time: 85.1 us; the launch traced here: 84.9 us
  Pallas kernels  79.8 us (94%)
  local copies, waits for them, and re-layouts  4.52 us (5%)
    pallas_call x1, Pallas kernels, body(): pl.pallas_call(kernel, out_shape=[jax.ShapeDtypeStruct((2048, 128), F32)]...  79.8 us
    unnamed x2, local copies, waits for them, and re-layouts  4.52 us

profile of v5, /device:TPU:1, one launch (start us, length us, event | category | flops | bytes accessed | tf_op | source)
XLA Modules:
  0.0 84.9 jit_solution(4515833521085290234)
XLA Ops:
  0.6 79.8 %shard_map.95 = (f32[2048,128]{1,0:T(8,128)}, f32[2048,128]{1,0:T(8,128)}) custom-call(f32[512,128]{1,0:T(8,128)} %bitcast.23, f32[512,128]{1,0:T(8,128)} %bitcast.24, f32[6,4,64,256]{3,2,1,0:T(8,128)} %lower_hbm.1, f32[6,4,64,256]{3,2,1,0:T(8,128)} %upper_hbm.1, f32[4,4,256,256]{3,2,1,0:T(8,128)} %linv_hbm.1, f32[4,4,256,256]{3,2,1,0:T(8,128)} %uinv_hbm.1, ...), custom_call_target="tpu_custom_call" | custom-call | tf_op jit(solution)/shard_map/pallas_call | solution.py:609
  80.4 2.3 %copy.16 = f32[4,4,16384]{2,1,0:T(4,128)} copy(f32[4,4,16384]{2,1,0:T(4,128)} %bitcast.22) | data formatting | bytes 2097152
  82.7 2.3 %copy.17 = f32[4,4,16384]{2,1,0:T(4,128)} copy(f32[4,4,16384]{2,1,0:T(4,128)} %bitcast.21) | data formatting | bytes 2097152

commit v6 on v5

--- a/solution.py
+++ b/solution.py
@@ -11,12 +11,12 @@
 LANES = 128
 PART = 64
 NODES_HERE = 4
-OFFSETS = sorted(
-    [(dz, dy) for dz in range(4) for dy in range(4) if dz or dy],
-    key=lambda o: -(min(o[0], 4 - o[0]) + min(o[1], 4 - o[1])),
-)
+OFFSETS = [
+    (2, 2), (1, 2), (2, 3), (3, 1), (0, 2), (3, 3), (1, 3), (2, 1), (3, 2), (1, 1),
+    (2, 0), (1, 0), (0, 1), (0, 3), (3, 0),
+]
 INPUT, SCATTER, GATHER, RHS, F_GZ, Y_ROW, Y_GZ, PX = 0, 1, 4, 7, 11, 15, 19, 22
-L_NEAR, L_FAR, L_GZ, U_NEAR, U_FAR, U_GZ, TOP_IN, NEXT_IN, PHASES = 25, 28, 31, 34, 40, 46, 52, 53, 54
+L_NEAR, L_FAR, L_GZ, U_NEAR, U_FAR, U_GZ, TOP_IN, NEXT_IN, OWN, PHASES = 25, 28, 31, 34, 40, 46, 52, 53, 54, 55
 
 
 def place_of(height, distance):
@@ -101,7 +101,7 @@
     fwd_hbm, bwd_hbm,
     right, sums, lower, lpart, upper, linv, uinv,
     topsend, toprecv, nextsend, nextrecv, xsend, xrecv, init, sbuf, qbuf, gbuf0, gbuf1, gbuf2, rbuf, pxsend, pxrecv,
-    full, fbuf, fown, ybuf, vpart, ownrhs, v21, v11, ul, w11, w21, w31, out_f, out_b,
+    full, fbuf, fown, ybuf, vpart, v21, v11, ul, w11, w21, w31, out_f, out_b,
     send_sem, recv_sem, load_sem, store_sem,
 ):
     g = lax.axis_index("gz")
@@ -280,11 +280,7 @@
     def take_rhs(height):
         wait_blocks(recv_sem.at[RHS + height], 3)
         blocks = [rbuf[height, mate] for mate in range(4)]
-        if height == 2:
-            own = exchange(blocks)
-            for mate in range(4):
-                ownrhs[mate] = own[mate]
-        else:
+        if height < 2:
             blocks = exchange(blocks)
         return pair_of(jnp.concatenate(blocks, axis=0))
 
@@ -309,18 +305,23 @@
 
     def send_terms(height, distance, b_pair):
         place = height + distance - 4
-        total = part_terms(place, b_pair)
+        send_parts(place, PX + place, part_terms(place, b_pair))
+
+    def send_parts(place, phase, total):
         blocks = exchange([total[16 * part:16 * part + 16] for part in range(4)])
         for mate in range(4):
             pxsend[place, mate] = blocks[mate]
         pxrecv[place, r] = pxsend[place, r]
         for step in row_steps:
             to = (r + step) % 4
-            send(pxsend.at[place, to], pxrecv.at[place, r], PX + place, {"row": to})
+            send(pxsend.at[place, to], pxrecv.at[place, r], phase, {"row": to})
 
     def take_terms(height, distance):
         place = height + distance - 4
-        wait_bytes(pxrecv.at[place, pl.ds(0, 3)], recv_sem.at[PX + place])
+        return take_parts(place, PX + place)
+
+    def take_parts(place, phase):
+        wait_bytes(pxrecv.at[place, pl.ds(0, 3)], recv_sem.at[phase])
         return jnp.concatenate(exchange([pxrecv[place, mate] for mate in range(4)]), axis=0)
 
     def finish_forward(height, b_pair):
@@ -477,7 +478,9 @@
     multiply(v21, lambda m: lower[1, m], lambda m: linv[2, m])
     scatter_terms(3, 2, take_terms(3, 2), True, False)
 
-    spread_rhs(2, sum_received(2))
+    rhs = sum_received(2)
+    send_parts(3, OWN, rhs)
+    spread_rhs(2, rhs)
     l_far(1)
     scatter_terms(3, 3, take_terms(3, 3), True, False)
     wait_bytes(xrecv.at[pl.ds(0, 7)], recv_sem.at[INPUT])
@@ -485,8 +488,8 @@
     for height in range(2):
         for parity in range(2):
             init[height, pl.ds(parity, 32, stride=2), :] = half_of(parts, parity, height)
+    scatter_terms(2, 1, apply(lambda m: v21[m], operand_of(take_parts(3, OWN))), False, True)
     b_pair = take_rhs(2)
-    scatter_terms(2, 1, apply(lambda m: v21[m], operand_of(ownrhs[r])), False, True)
     send_terms(2, 2, b_pair)
     u_far(0)
     u_near(2)
@@ -588,8 +591,8 @@
     ):
         wait_blocks(send_sem.at[phase], blocks)
     wait_bytes(xrecv.at[pl.ds(0, 7)], send_sem.at[INPUT])
-    for place in range(3):
-        wait_bytes(pxrecv.at[place, pl.ds(0, 3)], send_sem.at[PX + place])
+    for phase in (PX, PX + 1, PX + 2, OWN):
+        wait_bytes(pxrecv.at[0, pl.ds(0, 3)], send_sem.at[phase])
     for slot, (height, out, hbm) in enumerate(
         [(h, out_f, fwd_hbm) for h in (3, 2, 1, 0)] + [(h, out_b, bwd_hbm) for h in (0, 1, 2, 3)]
     ):
@@ -632,14 +635,13 @@
             pltpu.VMEM((16, 64, 128), F32),
             pltpu.VMEM((16, 64, 128), F32),
             pltpu.VMEM((3, 4, 64, 128), F32),
-            pltpu.VMEM((3, 4, 16, 128), F32),
-            pltpu.VMEM((3, 4, 16, 128), F32),
+            pltpu.VMEM((4, 4, 16, 128), F32),
+            pltpu.VMEM((4, 4, 16, 128), F32),
             pltpu.VMEM((256, 128), F32),
             pltpu.VMEM((4, 2, 256, 128), F32),
             pltpu.VMEM((3, 4, 64, 128), F32),
             pltpu.VMEM((4, 8, 64, 128), F32),
             pltpu.VMEM((4, 4, 64, 256), F32),
-            pltpu.VMEM((4, 64, 128), F32),
         ]
         + [pltpu.VMEM((4, 256, 512), BF16)] * 6
         + [
@@ -658,6 +660,26 @@
         upper_diagonal_inverses, pattern.T, parents,
     )
 
+    def copy_out(f_in, b_in, f_to, b_to, sems):
+        moves = []
+        for source, target in ((f_in, f_to), (b_in, b_to)):
+            for part in range(4):
+                rows = pl.ds(part * 512, 512)
+                moves.append(pltpu.make_async_copy(source.at[rows], target.at[rows], sems.at[len(moves)]))
+        for move in moves:
+            move.start()
+        for move in moves:
+            move.wait()
+
+    forward, backward = pl.pallas_call(
+        copy_out,
+        out_shape=[jax.ShapeDtypeStruct((2048, 128), F32)] * 2,
+        in_specs=[anywhere] * 2,
+        out_specs=[pl.BlockSpec(memory_space=pltpu.HBM)] * 2,
+        scratch_shapes=[pltpu.SemaphoreType.DMA((8,))],
+        compiler_params=pltpu.CompilerParams(vmem_limit_bytes=8 * 1024 * 1024),
+    )(forward, backward)
+
     def untiled(x):
         return x.reshape(4, 128, 4, 128).transpose(0, 2, 1, 3).reshape(4, 4, 16384)
 

time: 85.1 us -> 83.5 us (0.981)
  local copies, waits for them, and re-layouts: 4.52 us -> 2.44 us
    unnamed x2 -> x4, local copies, waits for them, and re-layouts: 4.52 us -> 2.44 us
    pallas_call x0 -> x1, Pallas kernels: none -> 1.37 us  [body(): pl.pallas_call(copy_out, out_shape=[jax.ShapeDtypeStruct((2048, 128), F32...]
    pallas_call x1, Pallas kernels: 79.8 us -> 78.7 us  [body(): pl.pallas_call(kernel, out_shape=[jax.ShapeDtypeStruct((2048, 128), F32)]...]
where the time goes in v6:
time: 83.5 us; the launch traced here: 83.3 us
  Pallas kernels  80.1 us (96%)
  local copies, waits for them, and re-layouts  2.44 us (3%)
    pallas_call x1, Pallas kernels, body(): pl.pallas_call(kernel, out_shape=[jax.ShapeDtypeStruct((2048, 128), F32)]...  78.7 us
    unnamed x4, local copies, waits for them, and re-layouts  2.44 us

profile of v6, /device:TPU:1, one launch (start us, length us, event | category | flops | bytes accessed | tf_op | source)
XLA Modules:
  0.0 83.3 jit_solution(10140621645040878462)
XLA Ops:
  0.6 78.7 %shard_map.95 = (f32[2048,128]{1,0:T(8,128)}, f32[2048,128]{1,0:T(8,128)}) custom-call(f32[512,128]{1,0:T(8,128)} %bitcast.21, f32[512,128]{1,0:T(8,128)} %bitcast.22, f32[6,4,64,256]{3,2,1,0:T(8,128)} %lower_hbm.1, f32[6,4,64,256]{3,2,1,0:T(8,128)} %upper_hbm.1, f32[4,4,256,256]{3,2,1,0:T(8,128)} %linv_hbm.1, f32[4,4,256,256]{3,2,1,0:T(8,128)} %uinv_hbm.1, ...), custom_call_target="tpu_custom_call" | custom-call | tf_op jit(solution)/shard_map/pallas_call | solution.py:612
  79.3 0.0 copy-start
  79.4 1.2 %copy-done = f32[2048,128]{1,0:T(8,128)S(1)} copy-done((f32[2048,128]{1,0:T(8,128)S(1)}, f32[2048,128]{1,0:T(8,128)}, u32[]{:S(2)}) %copy-start) | copy-done | bytes 1048600
  80.6 0.0 copy-start.1
  80.6 1.2 %copy-done.1 = f32[2048,128]{1,0:T(8,128)S(1)} copy-done((f32[2048,128]{1,0:T(8,128)S(1)}, f32[2048,128]{1,0:T(8,128)}, u32[]{:S(2)}) %copy-start.1) | copy-done | bytes 1048600
  81.8 1.4 %shard_map.96 = (f32[2048,128]{1,0:T(8,128)}, f32[2048,128]{1,0:T(8,128)}) custom-call(f32[2048,128]{1,0:T(8,128)S(1)} %copy-done, f32[2048,128]{1,0:T(8,128)S(1)} %copy-done.1), custom_call_target="tpu_custom_call" | custom-call | tf_op jit(solution)/shard_map/pallas_call | solution.py:674
Async XLA Ops:
  79.3 1.2 %copy-start = (f32[2048,128]{1,0:T(8,128)S(1)}, f32[2048,128]{1,0:T(8,128)}, u32[]{:S(2)}) copy-start(f32[2048,128]{1,0:T(8,128)} %get-tuple-element.6.f_in) | copy-start | bytes 3145732
  80.6 1.2 %copy-start.1 = (f32[2048,128]{1,0:T(8,128)S(1)}, f32[2048,128]{1,0:T(8,128)}, u32[]{:S(2)}) copy-start(f32[2048,128]{1,0:T(8,128)} %get-tuple-element.7.b_in) | copy-start | bytes 3145732

commit v7 on v6

--- a/solution.py
+++ b/solution.py
@@ -653,11 +653,17 @@
             pltpu.SemaphoreType.DMA((8,)),
         ],
         compiler_params=pltpu.CompilerParams(
-            collective_id=0, has_side_effects=True, vmem_limit_bytes=58 * 1024 * 1024
+            collective_id=0, has_side_effects=True, vmem_limit_bytes=50 * 1024 * 1024
         ),
     )(
-        tiled(right_side), tiled(layer_sums[0]), lower_blocks, upper_blocks, lower_inverse,
-        upper_diagonal_inverses, pattern.T, parents,
+        *[
+            pltpu.with_memory_space_constraint(x, pltpu.HBM)
+            for x in (
+                tiled(right_side), tiled(layer_sums[0]), lower_blocks, upper_blocks,
+                lower_inverse, upper_diagonal_inverses,
+            )
+        ],
+        pattern.T, parents,
     )
 
     def copy_out(f_in, b_in, f_to, b_to, sems):

time: 83.5 us -> 81.7 us (0.978)
  local copies, waits for them, and re-layouts: 2.44 us -> 1.36 us
    unnamed x4, local copies, waits for them, and re-layouts: 2.44 us -> 1.36 us
where the time goes in v7:
time: 81.7 us; the launch traced here: 81.6 us
  Pallas kernels  79.4 us (97%)
  local copies, waits for them, and re-layouts  1.36 us (2%)
    pallas_call x1, Pallas kernels, body(): pl.pallas_call(kernel, out_shape=[jax.ShapeDtypeStruct((2048, 128), F32)]...  78 us

profile of v7, /device:TPU:1, one launch (start us, length us, event | category | flops | bytes accessed | tf_op | source)
XLA Modules:
  0.0 81.6 jit_solution(15967943522524050630)
XLA Ops:
  0.6 0.0 copy-start
  0.6 0.7 copy-done
  1.3 0.0 copy-start.1
  1.3 0.7 copy-done.1
  2.0 78.0 %shard_map.95 = (f32[2048,128]{1,0:T(8,128)S(1)}, f32[2048,128]{1,0:T(8,128)S(1)}) custom-call(f32[512,128]{1,0:T(8,128)} %bitcast.22, f32[512,128]{1,0:T(8,128)} %bitcast.23, f32[6,4,64,256]{3,2,1,0:T(8,128)} %lower_hbm.1, f32[6,4,64,256]{3,2,1,0:T(8,128)} %upper_hbm.1, f32[4,4,256,256]{3,2,1,0:T(8,128)} %linv_hbm.1, f32[4,4,256,256]{3,2,1,0:T(8,128)} %uinv_hbm.1, ...), custom_call_target="tpu_custom_call" | custom-call | tf_op jit(solution)/shard_map/pallas_call | solution.py:612
  80.0 1.4 %shard_map.96 = (f32[2048,128]{1,0:T(8,128)}, f32[2048,128]{1,0:T(8,128)}) custom-call(f32[2048,128]{1,0:T(8,128)S(1)} %get-tuple-element.6.f_in, f32[2048,128]{1,0:T(8,128)S(1)} %get-tuple-element.7.b_in), custom_call_target="tpu_custom_call" | custom-call | tf_op jit(solution)/shard_map/pallas_call | solution.py:680
Async XLA Ops:
  0.6 0.7 copy-start
  1.3 0.7 copy-start.1

commit v8 on v7

--- a/solution.py
+++ b/solution.py
@@ -660,10 +660,9 @@
             pltpu.with_memory_space_constraint(x, pltpu.HBM)
             for x in (
                 tiled(right_side), tiled(layer_sums[0]), lower_blocks, upper_blocks,
-                lower_inverse, upper_diagonal_inverses,
+                lower_inverse, upper_diagonal_inverses, pattern.T, parents,
             )
         ],
-        pattern.T, parents,
     )
 
     def copy_out(f_in, b_in, f_to, b_to, sems):

time: 81.7 us -> 80.6 us (0.987)
  local copies, waits for them, and re-layouts: 1.36 us -> 0 us
    unnamed x4 -> x0, local copies, waits for them, and re-layouts: 1.36 us -> none
where the time goes in v8:
time: 80.6 us; the launch traced here: 80.4 us
  Pallas kernels  79.6 us (99%)
    pallas_call x1, Pallas kernels, body(): pl.pallas_call(kernel, out_shape=[jax.ShapeDtypeStruct((2048, 128), F32)]...  78.3 us

profile of v8, /device:TPU:1, one launch (start us, length us, event | category | flops | bytes accessed | tf_op | source)
XLA Modules:
  0.0 80.4 jit_solution(10843506699905757795)
XLA Ops:
  0.6 78.3 %shard_map.95 = (f32[2048,128]{1,0:T(8,128)S(1)}, f32[2048,128]{1,0:T(8,128)S(1)}) custom-call(f32[512,128]{1,0:T(8,128)} %bitcast.21, f32[512,128]{1,0:T(8,128)} %bitcast.22, f32[6,4,64,256]{3,2,1,0:T(8,128)} %lower_hbm.1, f32[6,4,64,256]{3,2,1,0:T(8,128)} %upper_hbm.1, f32[4,4,256,256]{3,2,1,0:T(8,128)} %linv_hbm.1, f32[4,4,256,256]{3,2,1,0:T(8,128)} %uinv_hbm.1, ...), custom_call_target="tpu_custom_call" | custom-call | tf_op jit(solution)/shard_map/pallas_call | solution.py:612
  78.9 1.4 %shard_map.96 = (f32[2048,128]{1,0:T(8,128)}, f32[2048,128]{1,0:T(8,128)}) custom-call(f32[2048,128]{1,0:T(8,128)S(1)} %get-tuple-element.6.f_in, f32[2048,128]{1,0:T(8,128)S(1)} %get-tuple-element.7.b_in), custom_call_target="tpu_custom_call" | custom-call | tf_op jit(solution)/shard_map/pallas_call | solution.py:679
